TPU v7x, 512 devices: a whole 4x8x8 slice. The times are simulated.
512 devices in a mesh: seg: 16 (over y, core), band: 32 (over z, x).
Axes of the slice: x: 4, y: 8, z: 8, core: 2. Of those that a mesh axis runs over, the one named last changes fastest.
Arguments:
- sft: bfloat16 [32, 2, 2, 8192], P('seg', None, None, 'band'), may hold values from -6 to 6
- doppler: float32 [32, 512], P('seg'), may hold values from -16 to 16
- antenna: float32 [32, 2, 2, 512], P('seg'), may hold values from -1 to 1
- coarse_index: int32 [32, 512], P('seg'), may hold values from 0 to 511
- freq_offset: int32 [32, 512], P('seg'), may hold values from -32 to 32
- wing_width: int32 [32], replicated, may hold values from 8 to 32
Outputs:
- fstat: float32 [512, 8192], P('seg', 'band')
All inputs are finite; a program needn't handle non-finite values.
Results may differ from a plain program's by a relative error of at most 0.00088.
Values may be sent and summed in bfloat16 or wider, within the bound.
No kernel may reach another device: no remote copies, remote signals or barrier semaphores. Data moves between devices by JAX's collectives and lax.ppermute only.
A program may use at most 64 MiB of HBM per device.

v0:
```python
import math

import jax
import jax.numpy as jnp
from jax import lax
from jax.sharding import PartitionSpec as P

WMAX = 32
OMAX = 32


def with_halo(block, sides, width):
    for axis, dim in sides:
        count = lax.axis_size(axis)
        forward = [(i, i + 1) for i in range(count - 1)]
        backward = [(target, source) for source, target in forward]
        low = lax.ppermute(
            lax.slice_in_dim(block, block.shape[dim] - width, None, axis=dim), axis, forward
        )
        high = lax.ppermute(lax.slice_in_dim(block, 0, width, axis=dim), axis, backward)
        block = jnp.concatenate([low, block, high], axis=dim)
    return block


def kernel_block(shifts, weights):
    tap_pos = jnp.arange(2 * WMAX).astype(jnp.float32) - WMAX
    offsets = tap_pos[None, None, :] - shifts[:, :, None]
    envelope = jnp.sinc(offsets)
    real_part = envelope * jnp.cos(jnp.pi * offsets)
    imag_part = -envelope * jnp.sin(jnp.pi * offsets)
    from_real = jnp.stack([real_part, imag_part], -1)
    from_imag = jnp.stack([-imag_part, real_part], -1)
    stacked = jnp.transpose(jnp.stack([from_real, from_imag], 1), (0, 1, 3, 2, 4))
    antenna_t = jnp.transpose(weights, (0, 2, 3, 1))
    product = antenna_t[:, :, None, None, :, :, None] * stacked[:, None, :, :, :, None, :]
    count_seg = shifts.shape[0]
    return product.astype(jnp.bfloat16).reshape(count_seg, -1, shifts.shape[1] * 4)


def coarse_stat(padded, doppler, antenna, wing_width, first_bin, bin_count, band_bins):
    segs_here = padded.shape[0]
    tap_count = 2 * WMAX
    unfolded = jnp.stack(
        [padded[:, :, :, column : column + bin_count] for column in range(tap_count)], axis=3
    )
    global_bin = first_bin + jnp.arange(bin_count)
    subband = global_bin // band_bins
    member = subband[:, None] == jnp.arange(wing_width.shape[0])[None, :]
    wing_reach = jnp.sum(jnp.where(member, wing_width[None, :], 0), axis=1)
    tap_index = jnp.arange(tap_count) - WMAX
    inside = (tap_index[:, None] >= -wing_reach[None, :]) & (
        tap_index[:, None] < wing_reach[None, :]
    )
    unfolded = unfolded * inside.astype(jnp.bfloat16)
    unfolded = unfolded.reshape(segs_here, -1, bin_count)
    coarse_count = doppler.shape[1]
    block_size = math.gcd(coarse_count, 256 >> min(3, (segs_here // 4).bit_length()))
    blocks = coarse_count // block_size
    shift_blocks = jnp.moveaxis(doppler.reshape(segs_here, blocks, block_size), 1, 0)
    weight_blocks = jnp.moveaxis(
        antenna.reshape(segs_here, 2, antenna.shape[2], blocks, block_size), 3, 0
    )

    def one_block(block_args):
        kernel = kernel_block(block_args[0], block_args[1])
        amplitude = jnp.einsum("skf,skn->snf", unfolded, kernel, preferred_element_type=jnp.float32)
        amplitude = amplitude.reshape(segs_here, block_size, 4, bin_count)
        return 0.25 * jnp.sum(amplitude * amplitude, axis=2)

    result = lax.map(one_block, (shift_blocks, weight_blocks))
    return jnp.transpose(result, (1, 0, 2, 3)).reshape(segs_here, coarse_count, bin_count)


def fine_sums(coarse, coarse_index, freq_offset, width):
    window = jax.vmap(
        lambda row_data, shift_bins: lax.dynamic_slice_in_dim(row_data, shift_bins + OMAX, width)
    )

    def add_segment(partial_sum, inputs):
        segment_coarse, indices, offsets = inputs
        picked = jnp.take(segment_coarse, indices, axis=0)
        return (partial_sum + window(picked, offsets), None)

    initial = jnp.zeros((coarse_index.shape[1], width), jnp.float32)
    total, unused = lax.scan(add_segment, initial, (coarse, coarse_index, freq_offset))
    return total


def per_device(sft, doppler, antenna, coarse_index, freq_offset, wing_width):
    band_bins = sft.shape[3]
    band_start = lax.axis_index("band") * band_bins
    seg_count = lax.axis_size("seg")
    total_segments = sft.shape[0] * seg_count
    padded = with_halo(sft, (("band", 3),), WMAX)
    inner = coarse_stat(padded, doppler, antenna, wing_width, band_start, band_bins, band_bins)
    coarse = with_halo(inner, (("band", 2),), OMAX)
    partial_sum = fine_sums(coarse, coarse_index, freq_offset, band_bins)
    summed = lax.psum_scatter(partial_sum, "seg", scatter_dimension=0, tiled=True)
    return summed * (1.0 / total_segments)


def solution(mesh):
    placed = (
        P("seg", None, None, "band"),
        P("seg", None),
        P("seg", None, None, None),
        P("seg", None),
        P("seg", None),
        P(),
    )
    return jax.shard_map(
        per_device, mesh=mesh, in_specs=placed, out_specs=P("seg", "band"), check_vma=False
    )
```

profile of v0, /device:TPU:27, one launch (start us, length us, event | category | flops | bytes accessed | tf_op | source)
XLA Modules:
  0.0 2179.4 jit_solution(4229016444096606403)
XLA Ops:
  7.3 3.1 collective-permute-start
  10.4 2.2 collective-permute-start.1
  43.2 29.4 %while.32 = (s32[]{:T(128)}, f32[2,2,256,256]{3,2,1,0:T(8,128)}, f32[2,2,2,2,256]{4,0,3,2,1:T(2,128)S(1)}, f32[2,2,256]{2,1,0:T(2,128)}, bf16[2,256,256]{2,1,0:T(8,128)(2,1)S(1)}) while((s32[]{:T(128)}, f32[2,2,256,256]{3,2,1,0:T(8,128)}, f32[2,2,2,2,256]{4,0,3,2,1:T(2,128)S(1)}, f32[2,2,256]{2,1,0:T(2,128)}, ...), condition=%wide.region_3.4_spmd.clone, body=%wide.region_1.3_spmd.sunk.clone | while | flops 272072832 | bytes 18398280 | solution.py:70
  46.5 4.3 multiply_convert_fusion.3
  50.8 1.4 convert_element_type.48
  52.2 1.8 convolution_multiply_fusion.3
  54.0 1.9 mul.726
  61.2 4.3 multiply_convert_fusion.3
  65.5 1.4 convert_element_type.48
  66.9 1.8 convolution_multiply_fusion.3
  68.7 1.9 mul.726
  72.6 1.3 copy.21
  74.2 3.3 collective-permute-start.2
  77.4 2.2 collective-permute-start.3
  79.6 8.9 collective-permute-done.2
  88.5 2.9 collective-permute-done.3
  91.4 1.6 pad_maximum_fusion
  93.1 2006.7 %while.34 = (s32[]{:T(128)}, f32[512,256]{1,0:T(8,128)}, s32[2,512]{1,0:T(2,128)S(1)}, f32[2,512,320]{2,1,0:T(8,128)S(1)}, s32[2,512]{1,0:T(2,128)S(1)}, /*index=5*/s32[]{:T(128)}, s32[]{:T(128)}, f32[]{:T(128)}) while((s32[]{:T(128)}, f32[512,256]{1,0:T(8,128)}, s32[2,512]{1,0:T(2,128)S(1)}, ...), condition=%wide.region_5.6_spmd.clone.clone, body=%wide.region_4.5_spmd.clone.sunk.clone | while | flops 434693 | bytes 5541136 | solution.py:85
  93.2 1.6 gather_fusion
  95.0 1000.0 %while.33 = (s32[]{:T(128)}, f32[512,320]{1,0:T(8,128)S(1)}, s32[512,2]{0,1:T(2,128)S(1)}, f32[512,256]{1,0:T(8,128)S(1)}, s32[]{:T(128)}, /*index=5*/s32[]{:T(128)}) while((s32[]{:T(128)}, f32[512,320]{1,0:T(8,128)S(1)}, s32[512,2]{0,1:T(2,128)S(1)}, f32[512,256]{1,0:T(8,128)S(1)}, s32[]{:T(128)}, /*index=5*/s32[]{:T(128)}) %tuple.96), condition=%wide.while_cond, body=%wide.while_body.sunk | while | flops 2 | bytes 4209 | solution.py:76
  95.6 1.3 dynamic-slice.7
  97.6 1.3 dynamic-slice.7
  99.5 1.3 dynamic-slice.7
  101.5 1.3 dynamic-slice.7
  103.5 1.3 dynamic-slice.7
  105.4 1.3 dynamic-slice.7
  107.4 1.3 dynamic-slice.7
  113.2 1.3 dynamic-slice.7
  115.2 1.3 dynamic-slice.7
  117.1 1.3 dynamic-slice.7
  119.1 1.3 dynamic-slice.7
  121.0 1.3 dynamic-slice.7
  123.0 1.3 dynamic-slice.7
  124.9 1.3 dynamic-slice.7
  132.8 1.3 dynamic-slice.7
  134.7 1.3 dynamic-slice.7
  136.7 1.3 dynamic-slice.7
  138.6 1.3 dynamic-slice.7
  140.6 1.3 dynamic-slice.7
  142.5 1.3 dynamic-slice.7
  144.5 1.3 dynamic-slice.7
  150.3 1.3 dynamic-slice.7
  152.3 1.3 dynamic-slice.7
  1096.0 1.6 gather_fusion
  1097.8 1000.0 %while.33 = (s32[]{:T(128)}, f32[512,320]{1,0:T(8,128)S(1)}, s32[512,2]{0,1:T(2,128)S(1)}, f32[512,256]{1,0:T(8,128)S(1)}, s32[]{:T(128)}, /*index=5*/s32[]{:T(128)}) while((s32[]{:T(128)}, f32[512,320]{1,0:T(8,128)S(1)}, s32[512,2]{0,1:T(2,128)S(1)}, f32[512,256]{1,0:T(8,128)S(1)}, s32[]{:T(128)}, /*index=5*/s32[]{:T(128)}) %tuple.96), condition=%wide.while_cond, body=%wide.while_body.sunk | while | flops 2 | bytes 4209 | solution.py:76
  2097.8 1.9 select_add_fusion.3
  2099.8 71.5 %reduce-scatter.2.cloned.1.call-done = f32[32,256]{1,0:T(8,128)} async-done(((f32[512,256]{1,0:T(8,128)}), f32[32,256]{1,0:T(8,128)}) %reduce-scatter.2.cloned.1.call-update) | async-done | bytes 32784 | tf_op jit(solution)/shard_map/reduce_scatter | solution.py:98
  2171.2 1.4 broadcast_multiply_fusion
  (4197 shorter events, 1997.1 us)
Async XLA Ops:
  6.5 2164.7 %reduce-scatter.2.cloned.1.call-start = ((), (), s32[]{:S(2)}) async-start(), calls=%async_computation.1 | async-start | bytes 557056 | tf_op jit(solution)/shard_map/reduce_scatter | solution.py:98
  7.3 7.6 collective-permute-start
  10.4 30.0 %collective-permute-start.1 = (bf16[2,2,2,32]{3,2,1,0:T(2,128)(2,1)S(1)}, bf16[2,2,2,32]{3,2,1,0:T(2,128)(2,1)S(1)}, u32[]{:S(2)}, u32[]{:S(2)}) collective-permute-start(bf16[2,2,2,32]{3,2,1,0:T(2,128)(2,1)S(1)} %get-tuple-element.221), channel_id=1, source_target_pairs={{1,0},{2,1},{3,2},{4,3},{5,4},{6,5},{7,6},{8,7},{9,8},{10,9},{11,1... | collective-permute-start | bytes 1544 | tf_op jit(solution)/shard_map/ppermute | solution.py:20
  74.1 18.9 copy-start
  74.1 18.9 copy-start.1
  74.2 14.4 collective-permute-start.2
  77.4 14.0 collective-permute-start.3
Sparse Core Ops, SparseCore 0:
  2099.9 71.2 reduce-scatter.1
where the time goes:
time: 2200 us; the launch traced here: 2180 us
  local copies, waits for them, and re-layouts  2010 us (91%)
  waiting for transfers between devices  83.3 us (4%)
  other arithmetic  46.2 us (2%)
    gather x4096, local copies, waits for them, and re-layouts  1980 us
    reduce_scatter x1, waiting for transfers between devices, per_device(): lax.psum_scatter(partial_sum, 'seg', scatter_dimension=0, tiled=True)  71.5 us

commit v1 on v0

v1 whole, which is shorter than its diff:
```python
import functools

import jax
import jax.numpy as jnp
from jax import lax
from jax.experimental import pallas as pl
from jax.experimental.pallas import tpu as pltpu
from jax.sharding import PartitionSpec as P

WMAX = 32
OMAX = 32
LANES = 128
HALO = WMAX + OMAX
SFT_ROWS = 24
PARAM_ROWS = 16
ROWS = SFT_ROWS + PARAM_ROWS
VMEM = pltpu.VMEM
F32 = jnp.float32
BF16 = jnp.bfloat16


def pieces(value):
    high = value.astype(BF16)
    rest = value - high.astype(F32)
    middle = rest.astype(BF16)
    low = (rest - middle.astype(F32)).astype(BF16)
    return high, middle, low


def lane_iota(shape):
    return lax.broadcasted_iota(jnp.int32, shape, len(shape) - 1)


def row_iota(shape):
    return lax.broadcasted_iota(jnp.int32, shape, len(shape) - 2)


def choose_params(doppler_ref, antenna_ref, index_ref, offset_ref, out_ref):
    coarse = doppler_ref.shape[1]
    fine = index_ref.shape[1]
    own = fine // out_ref.shape[0]
    per_tile = LANES // own
    lanes = lane_iota((PARAM_ROWS, LANES))
    tiles = []
    for seg in range(2):
        values = jnp.concatenate(
            [doppler_ref[seg : seg + 1, :]]
            + [antenna_ref[seg, q, d : d + 1, :] for q in range(2) for d in range(2)], 0
        )
        high, middle, low = pieces(values)
        table = jnp.concatenate(
            [high.astype(F32), middle.astype(F32), low.astype(F32), jnp.zeros((1, coarse), F32)], 0
        ).astype(BF16)
        hot = row_iota((coarse, fine)) == index_ref[seg : seg + 1, :]
        chosen = jnp.dot(table, jnp.where(hot, 1.0, 0.0).astype(BF16), preferred_element_type=F32)
        shift = jnp.broadcast_to(offset_ref[seg : seg + 1, :].astype(F32), chosen.shape)
        chosen = jnp.where(row_iota(chosen.shape) == PARAM_ROWS - 1, shift, chosen)
        tiles.append(chosen)
    for peer in range(out_ref.shape[0]):
        tile, place = divmod(peer, per_tile)
        cols = slice(tile * LANES, (tile + 1) * LANES)
        first = pltpu.roll(tiles[0][:, cols], (LANES - place * own) % LANES, 1)
        second = pltpu.roll(tiles[1][:, cols], (LANES - place * own + own) % LANES, 1)
        out_ref[peer] = jnp.where(lanes < own, first, second).astype(BF16)


def pack(left_ref, own_ref, right_ref, params_ref, out_ref):
    bins = own_ref.shape[3]
    rows = []
    for ref, start in ((left_ref, bins - HALO), (own_ref, 0), (right_ref, 0)):
        width = bins if ref is own_ref else HALO
        rows.append(jnp.concatenate(
            [ref[s, d, :, start : start + width].astype(F32) for s in range(2) for d in range(2)], 0
        ))
    padded = jnp.concatenate(rows, 1)
    mirror = jnp.where(
        row_iota((LANES, LANES)) + lane_iota((LANES, LANES)) == LANES - 1, 1.0, 0.0
    ).astype(BF16)
    chunks = jnp.concatenate(
        [padded[:, c * LANES : (c + 1) * LANES] for c in reversed(range(SFT_ROWS // 8))], 0
    ).astype(BF16)
    block = jnp.dot(chunks, mirror, preferred_element_type=F32).astype(BF16)
    for peer in range(out_ref.shape[0]):
        out_ref[peer, :SFT_ROWS, :] = block
        out_ref[peer, SFT_ROWS:, :] = params_ref[peer]


def fine_stat(scale, wing_ref, recv_ref, out_ref, x_ref, m_ref, edge_ref, t_ref, k_ref, acc_ref):
    peers = recv_ref.shape[0]
    fine, bins = out_ref.shape
    band = lax.axis_index("band")
    last = lax.axis_size("band") - 1
    w_own = wing_ref[band].astype(F32)
    w_prev = jnp.where(band > 0, wing_ref[jnp.maximum(band - 1, 0)], 0).astype(F32)
    w_next = jnp.where(band < last, wing_ref[jnp.minimum(band + 1, last)], 0).astype(F32)

    lanes16 = lane_iota((peers, LANES))
    part = lambda i: recv_ref[:, SFT_ROWS + i, :].astype(F32)
    whole = lambda i: part(i) + part(5 + i) + part(10 + i)
    doppler = whole(0)
    shift = part(PARAM_ROWS - 1)
    frac = doppler - jnp.round(doppler)
    factor = jnp.sin(jnp.pi * frac) * (1.0 / jnp.pi)
    wing = jnp.where(shift < 0, w_prev, w_next)
    for i, row in enumerate([doppler, shift, factor, wing, whole(1), whole(2), whole(3), whole(4)]):
        m_ref[:, i, :] = row
    for seg in range(2):
        group = jnp.where(lanes16 // fine == seg, shift, 0.0)
        group = group + pltpu.roll(group, 2 * fine, 1)
        group = group + pltpu.roll(group, fine, 1)
        edge_ref[:, seg, :] = group
    acc_ref[...] = jnp.zeros_like(acc_ref)

    tap = (HALO - 1) - lane_iota((fine, LANES)).astype(F32)
    bend = lane_iota((16, LANES)) - row_iota((16, LANES))
    lane = lane_iota((OMAX, LANES))
    row = row_iota((OMAX, LANES)).astype(F32)
    other = lane >= LANES // 2

    @pl.loop(0, peers)
    def _(peer):
        x_ref[...] = recv_ref[peer, :SFT_ROWS, :].astype(F32)
        columns = m_ref[peer].T
        for seg in range(2):
            here = columns[seg * fine : (seg + 1) * fine, :]
            col = lambda i: jnp.broadcast_to(here[:, i : i + 1], (fine, LANES))
            offset = col(1)
            k = tap - offset
            u = k - col(0)
            envelope = jnp.where(u == 0, 1.0, col(2) / jnp.where(u == 0, 1.0, u))
            middle = jnp.abs(k + 0.5)
            for v, width in ((0, w_own), (1, col(3))):
                masked = jnp.where(middle < width, envelope, 0.0)
                for q in range(2):
                    for d in range(2):
                        at = (v * 2 + q) * fine
                        k_ref[seg, at : at + fine, d * LANES : (d + 1) * LANES] = (
                            masked * col(4 + q * 2 + d)
                        ).astype(BF16)
            for d in range(2):
                for ri in range(2):
                    at = seg * 4 + d * 2 + ri
                    spread = [
                        jnp.broadcast_to(x_ref[c * 8 + at : c * 8 + at + 1, :], (16, LANES))
                        for c in range(SFT_ROWS // 8)
                    ]
                    for a in range(1, LANES // 16 + 1):
                        turned = [
                            pltpu.roll(s, LANES - 16 * a, 1, stride=1, stride_axis=0)
                            for s in spread
                        ]
                        inside = bend < LANES - 16 * a
                        for c in range(bins // LANES):
                            start = (ri + 1) * bins - c * LANES - 16 * a
                            t_ref[seg, start : start + 16, d * LANES : (d + 1) * LANES] = jnp.where(
                                inside, turned[c], turned[c + 1]
                            ).astype(BF16)
            amp = lax.dot_general(
                t_ref[seg], k_ref[seg], (((1,), (1,)), ((), ())), preferred_element_type=F32
            )
            power = amp[:bins] * amp[:bins] + amp[bins:] * amp[bins:]
            edge = edge_ref[peer, seg : seg + 1, :]
            low_ok = (row >= -edge) != other
            high_ok = (row < OMAX - edge) != other
            acc_ref[:OMAX, :] += jnp.where(low_ok, power[:OMAX], 0.0)
            acc_ref[OMAX : bins - OMAX, :] += power[OMAX : bins - OMAX]
            acc_ref[bins - OMAX :, :] += jnp.where(high_ok, power[bins - OMAX :], 0.0)

    f = row_iota((bins, LANES))
    keep = (lane_iota((bins, LANES)) < LANES // 2) | (f < OMAX) | (f >= bins - OMAX)
    total = jnp.where(keep, acc_ref[...], 0.0)
    total = total + pltpu.roll(total, LANES // 2, 1)
    total = total + pltpu.roll(total, LANES // 4, 1)
    out_ref[...] = total.T[:fine, :] * scale


def per_device(sft, doppler, antenna, coarse_index, freq_offset, wing_width):
    bins = sft.shape[3]
    peers = lax.axis_size("seg")
    count = lax.axis_size("band")
    fine = coarse_index.shape[1] // peers
    segments = sft.shape[0] * peers
    up = [(i, i + 1) for i in range(count - 1)]
    left = lax.ppermute(sft, "band", up)
    right = lax.ppermute(sft, "band", [(b, a) for a, b in up])
    params = pl.pallas_call(
        choose_params,
        out_shape=jax.ShapeDtypeStruct((peers, PARAM_ROWS, LANES), BF16),
        name="choose_params",
    )(doppler, antenna, coarse_index, freq_offset)
    sent = pl.pallas_call(
        pack, out_shape=jax.ShapeDtypeStruct((peers, ROWS, LANES), BF16), name="pack"
    )(left, sft, right, params)
    recv = lax.all_to_all(sent, "seg", 0, 0, tiled=True)
    return fine_call(recv, wing_width, fine, bins, peers, segments)


def fine_call(recv, wing_width, fine, bins, peers, segments):
    return pl.pallas_call(
        functools.partial(fine_stat, 1.0 / (4 * segments)),
        out_shape=jax.ShapeDtypeStruct((fine, bins), F32),
        in_specs=[pl.BlockSpec(memory_space=pltpu.SMEM), pl.BlockSpec(memory_space=VMEM)],
        scratch_shapes=[
            VMEM((SFT_ROWS, LANES), F32),
            VMEM((peers, 8, LANES), F32),
            VMEM((peers, 2, LANES), F32),
            VMEM((2, 2 * bins, 2 * LANES), BF16),
            VMEM((2, 4 * fine, 2 * LANES), BF16),
            VMEM((bins, LANES), F32),
        ],
        name="fine_stat",
    )(wing_width, recv)


def solution(mesh):
    placed = (
        P("seg", None, None, "band"),
        P("seg", None),
        P("seg", None, None, None),
        P("seg", None),
        P("seg", None),
        P(),
    )
    return jax.shard_map(
        per_device, mesh=mesh, in_specs=placed, out_specs=P("seg", "band"), check_vma=False
    )
```

time: 2200 us -> 47.2 us (0.02)
  the two profiles are of different devices: /device:TPU:27 before, /device:TPU:199 now
where the time goes in v1:
time: 47.2 us; the launch traced here: 46.8 us
  blocking collectives  18.8 us (40%)
  Pallas kernels  16.1 us (34%)
  starting transfers between devices  7.04 us (15%)
  waiting for transfers between devices  4.25 us (9%)
  local copies, waits for them, and re-layouts  0.6 us (1%)
    all_to_all x1, blocking collectives, per_device(): recv = lax.all_to_all(sent, 'seg', 0, 0, tiled=True)  18.8 us
    pallas_call x1, Pallas kernels, fine_call(): pl.pallas_call(functools.partial(fine_stat, 1.0 / (4 * segments)), out_sh...  12.7 us
    ppermute x1, starting transfers between devices, per_device(): left = lax.ppermute(sft, 'band', up)  5.12 us
    ppermute x1, waiting for transfers between devices, per_device(): right = lax.ppermute(sft, 'band', [(b, a) for a, b in up])  4.25 us
    ppermute x1, starting transfers between devices, per_device(): right = lax.ppermute(sft, 'band', [(b, a) for a, b in up])  1.92 us
    pallas_call x1, Pallas kernels, per_device(): pl.pallas_call(pack, out_shape=jax.ShapeDtypeStruct((peers, ROWS, LANES),...  1.74 us
    pallas_call x1, Pallas kernels, per_device(): pl.pallas_call(choose_params, out_shape=jax.ShapeDtypeStruct((peers, PARA...  1.7 us
  transfers between devices with their start and end apart: 2, of which 1 were waited for; matrix products, arithmetic and copies ran while one was open for 0% of the time, Pallas kernels for 4%

profile of v1, /device:TPU:199, one launch (start us, length us, event | category | flops | bytes accessed | tf_op | source)
XLA Modules:
  0.0 46.8 jit_solution(10041169830494749984)
XLA Ops:
  0.0 5.1 %collective-permute-start = (bf16[2,2,2,256]{3,2,1,0:T(2,128)(2,1)}, bf16[2,2,2,256]{3,2,1,0:T(2,128)(2,1)S(1)}, u32[]{:S(2)}, u32[]{:S(2)}) collective-permute-start(bf16[2,2,2,256]{3,2,1,0:T(2,128)(2,1)} %own_ref.1), channel_id=1, source_target_pairs={{0,1},{1,2},{2,3},{3,4},{4,5},{5,6},{6,7},{7,8},{8,9},{9,10},{10,1... | collective-permute-start | bytes 12296 | tf_op jit(solution)/shard_map/ppermute | solution.py:184
  5.1 1.9 %collective-permute-start.1 = (bf16[2,2,2,256]{3,2,1,0:T(2,128)(2,1)}, bf16[2,2,2,256]{3,2,1,0:T(2,128)(2,1)S(1)}, u32[]{:S(2)}, u32[]{:S(2)}) collective-permute-start(bf16[2,2,2,256]{3,2,1,0:T(2,128)(2,1)} %own_ref.1), channel_id=1, source_target_pairs={{1,0},{2,1},{3,2},{4,3},{5,4},{6,5},{7,6},{8,7},{9,8},{10,9},{11,1... | collective-permute-start | bytes 12296 | tf_op jit(solution)/shard_map/ppermute | solution.py:185
  7.1 1.7 %choose_params.1.params_ref = bf16[16,16,128]{2,1,0:T(8,128)(2,1)} custom-call(f32[2,512]{1,0:T(2,128)} %doppler_ref.1, f32[2,2,2,512]{3,2,1,0:T(2,128)} %antenna_ref.1, s32[2,512]{1,0:T(2,128)} %index_ref.1, s32[2,512]{1,0:T(2,128)} %offset_ref.1), custom_call_target="tpu_custom_call" | custom-call | tf_op jit(solution)/shard_map/choose_params/pallas_call | solution.py:186
  8.8 0.0 collective-permute-done.left_ref
  8.8 0.0 copy-start
  8.8 4.2 %collective-permute-done.1.right_ref = bf16[2,2,2,256]{3,2,1,0:T(2,128)(2,1)S(1)} collective-permute-done((bf16[2,2,2,256]{3,2,1,0:T(2,128)(2,1)}, bf16[2,2,2,256]{3,2,1,0:T(2,128)(2,1)S(1)}, u32[]{:S(2)}, u32[]{:S(2)}) %collective-permute-start.1) | collective-permute-done | bytes 4128 | tf_op jit(solution)/shard_map/ppermute | solution.py:185
  13.0 0.0 copy-done
  13.0 0.0 copy-start.1
  13.0 0.6 %copy-done.1 = bf16[2,2,2,256]{3,2,1,0:T(2,128)(2,1)} copy-done((bf16[2,2,2,256]{3,2,1,0:T(2,128)(2,1)}, bf16[2,2,2,256]{3,2,1,0:T(2,128)(2,1)S(1)}, u32[]{:S(2)}) %copy-start.1) | copy-done | bytes 4120
  13.6 1.7 %pack.1 = bf16[16,40,128]{2,1,0:T(8,128)(2,1)} custom-call(bf16[2,2,2,256]{3,2,1,0:T(2,128)(2,1)} %copy-done, bf16[2,2,2,256]{3,2,1,0:T(2,128)(2,1)} %own_ref.1, bf16[2,2,2,256]{3,2,1,0:T(2,128)(2,1)} %copy-done.1, bf16[16,16,128]{2,1,0:T(8,128)(2,1)} %choose_params.1.params_ref), custom_call_target="tpu_custom_call" | custom-call | tf_op jit(solution)/shard_map/pack/pallas_call | solution.py:191
  15.3 18.8 %all_to_all.5.recv_ref = bf16[16,40,128]{2,1,0:T(8,128)(2,1)} all-to-all(bf16[16,40,128]{2,1,0:T(8,128)(2,1)} %pack.1), channel_id=1, replica_groups=mesh['seg'=16,'band'=32] {'seg'}, dimensions={0} | all-to-all | bytes 327680 | tf_op jit(solution)/shard_map/all_to_all | solution.py:194
  34.2 12.7 %fine_stat.1 = f32[32,256]{1,0:T(8,128)} custom-call(s32[32]{0:T(128)} %wing_ref.1, bf16[16,40,128]{2,1,0:T(8,128)(2,1)} %all_to_all.5.recv_ref), custom_call_target="tpu_custom_call" | custom-call | tf_op jit(solution)/shard_map/fine_stat/pallas_call | solution.py:199
Async XLA Ops:
  0.0 8.8 %collective-permute-start = (bf16[2,2,2,256]{3,2,1,0:T(2,128)(2,1)}, bf16[2,2,2,256]{3,2,1,0:T(2,128)(2,1)S(1)}, u32[]{:S(2)}, u32[]{:S(2)}) collective-permute-start(bf16[2,2,2,256]{3,2,1,0:T(2,128)(2,1)} %own_ref.1), channel_id=1, source_target_pairs={{0,1},{1,2},{2,3},{3,4},{4,5},{5,6},{6,7},{7,8},{8,9},{9,10},{10,1... | collective-permute-start | bytes 12296 | tf_op jit(solution)/shard_map/ppermute | solution.py:184
  5.1 7.9 %collective-permute-start.1 = (bf16[2,2,2,256]{3,2,1,0:T(2,128)(2,1)}, bf16[2,2,2,256]{3,2,1,0:T(2,128)(2,1)S(1)}, u32[]{:S(2)}, u32[]{:S(2)}) collective-permute-start(bf16[2,2,2,256]{3,2,1,0:T(2,128)(2,1)} %own_ref.1), channel_id=1, source_target_pairs={{1,0},{2,1},{3,2},{4,3},{5,4},{6,5},{7,6},{8,7},{9,8},{10,9},{11,1... | collective-permute-start | bytes 12296 | tf_op jit(solution)/shard_map/ppermute | solution.py:185
  8.8 4.3 %copy-start = (bf16[2,2,2,256]{3,2,1,0:T(2,128)(2,1)}, bf16[2,2,2,256]{3,2,1,0:T(2,128)(2,1)S(1)}, u32[]{:S(2)}) copy-start(bf16[2,2,2,256]{3,2,1,0:T(2,128)(2,1)S(1)} %collective-permute-done.left_ref) | copy-start | bytes 12292
  13.0 0.6 %copy-start.1 = (bf16[2,2,2,256]{3,2,1,0:T(2,128)(2,1)}, bf16[2,2,2,256]{3,2,1,0:T(2,128)(2,1)S(1)}, u32[]{:S(2)}) copy-start(bf16[2,2,2,256]{3,2,1,0:T(2,128)(2,1)S(1)} %collective-permute-done.1.right_ref) | copy-start | bytes 12292

commit v2 on v0

v2 whole, which is shorter than its diff:
```python
import math

import jax
import jax.numpy as jnp
from jax import lax
from jax.experimental import pallas as pl
from jax.experimental.pallas import tpu as pltpu
from jax.sharding import PartitionSpec as P

WMAX = 32
OMAX = 32
LANES = 128
TAPS = 2 * WMAX
HALF = LANES // 2
VMEM = pltpu.VMEM
F32 = jnp.float32
BF16 = jnp.bfloat16


def lane_iota(shape):
    return lax.broadcasted_iota(jnp.int32, shape, len(shape) - 1)


def row_iota(shape):
    return lax.broadcasted_iota(jnp.int32, shape, len(shape) - 2)


def split(value, count):
    parts = []
    for _ in range(count):
        part = value.astype(BF16)
        parts.append(part)
        value = value - part.astype(F32)
    return parts


def sin_pi_over_pi(r):
    r2 = r * r
    total = jnp.zeros_like(r)
    for n in reversed(range(8)):
        total = total * r2 + (-1) ** n * math.pi ** (2 * n) / math.factorial(2 * n + 1)
    return total * r


def make_taps(doppler_ref, antenna_ref, index_ref, out_ref):
    coarse = doppler_ref.shape[1]
    fine = index_ref.shape[1]
    tap = (WMAX - 1) - row_iota((TAPS, LANES)).astype(F32)
    for seg in range(2):
        values = jnp.concatenate(
            [doppler_ref[seg : seg + 1, :]]
            + [antenna_ref[seg, q, d : d + 1, :] for q in range(2) for d in range(2)], 0
        )
        table = jnp.concatenate(
            [part.astype(F32) for part in split(values, 3)] + [jnp.zeros((1, coarse), F32)], 0
        ).astype(BF16)
        for tile in range(fine // LANES):
            cols = slice(tile * LANES, (tile + 1) * LANES)
            hot = row_iota((coarse, LANES)) == index_ref[seg : seg + 1, cols]
            chosen = jnp.dot(table, jnp.where(hot, 1.0, 0.0).astype(BF16), preferred_element_type=F32)
            whole = chosen[0:5] + chosen[5:10] + chosen[10:15]
            shift = whole[0:1]
            factor = sin_pi_over_pi(shift - jnp.round(shift))
            u = tap - shift
            envelope = jnp.where(u == 0, 1.0, factor / u)
            for q in range(2):
                at = (tile * 2 + q) * LANES
                for d in range(2):
                    high, low = split(envelope * whole[1 + q * 2 + d : 2 + q * 2 + d], 2)
                    out_ref[seg, d * TAPS : (d + 1) * TAPS, at : at + LANES] = high
                    out_ref[seg, (2 + d) * TAPS : (3 + d) * TAPS, at : at + LANES] = low


def segment_sums(
    wing_ref, offset_ref, left_ref, own_ref, right_ref, taps_ref, out_ref,
    chunk_ref, t_ref, p_ref, u_ref, v_ref, acc_ref
):
    bins = own_ref.shape[3]
    span = bins + 2 * OMAX
    blocks = span // 16
    band = lax.axis_index("band")
    last = lax.axis_size("band") - 1
    w_own = wing_ref[band].astype(F32)
    w_prev = jnp.where(band > 0, wing_ref[jnp.maximum(band - 1, 0)], 0).astype(F32)
    w_next = jnp.where(band < last, wing_ref[jnp.minimum(band + 1, last)], 0).astype(F32)

    mirror = jnp.where(
        row_iota((LANES, LANES)) + lane_iota((LANES, LANES)) == LANES - 1, 1.0, 0.0
    ).astype(BF16)

    def rows_of(ref, start):
        return jnp.concatenate(
            [ref[s, d, :, start : start + LANES].astype(F32) for s in range(2) for d in range(2)], 0
        )

    parts = [rows_of(right_ref, 0)]
    parts += [rows_of(own_ref, c * LANES) for c in reversed(range(bins // LANES))]
    parts += [rows_of(left_ref, bins - LANES)]
    flipped = jnp.dot(
        jnp.concatenate(parts, 0).astype(BF16), mirror, preferred_element_type=F32
    )
    swapped = pltpu.roll(flipped, HALF, 1)
    for i in range(len(parts)):
        chunk_ref[0, i] = flipped[8 * i : 8 * i + 8]
        chunk_ref[1, i] = swapped[8 * i : 8 * i + 8]

    lane = lane_iota((16, LANES))
    low_half = lane < HALF
    within = lane % HALF
    bend = within - row_iota((16, LANES))
    center = jnp.abs((WMAX - 0.5) - within.astype(F32))
    reach = [center < w for w in (w_prev, w_own, w_next)]

    def half_row(h, place, row):
        chunk, half = (h + 1) // 2, (h + 1) % 2
        return jnp.broadcast_to(chunk_ref[half ^ place, chunk, row : row + 1, :], (16, LANES))

    def build(seg):
        for ri in range(2):
            first, second = seg * 4 + ri, seg * 4 + 2 + ri
            halves = span // HALF
            for h in range(halves):
                source = jnp.where(low_half, half_row(h, 0, first), half_row(h, 1, second))
                after = jnp.where(low_half, half_row(h + 1, 0, second), half_row(h + 1, 1, first))
                for a in range(1, 5):
                    turn = LANES - 16 * a
                    window = jnp.where(
                        bend < HALF - 16 * a,
                        pltpu.roll(source, turn, 1, stride=1, stride_axis=0),
                        pltpu.roll(after, turn, 1, stride=1, stride_axis=0),
                    )
                    block = blocks - 4 * h - a
                    side = 0 if block < OMAX // 16 else (2 if block >= blocks - OMAX // 16 else 1)
                    window = jnp.where(reach[side], window, 0.0).astype(BF16)
                    start = block * 32 + ri * 16
                    t_ref[seg, start : start + 16, :LANES] = window
                    t_ref[seg, start : start + 16, LANES:] = window

    def moved(seg, tile, slot):
        amount = offset_ref[seg : seg + 1, tile * LANES : (tile + 1) * LANES] + OMAX
        bit = lambda b: jnp.broadcast_to((amount & b) != 0, (8, LANES))
        size = bins // 8
        tiles = [p_ref[slot, 8 * t : 8 * t + 8, :] for t in range(span // 8)]
        far = bit(64)
        tiles = [jnp.where(far, tiles[t + 8], tiles[t]) for t in range(size)] + tiles[size:]
        for b in (32, 16, 8):
            pick, step = bit(b), b // 8
            tiles = [jnp.where(pick, tiles[t + step], tiles[t]) for t in range(size + step)]
        for t, value in enumerate(tiles):
            u_ref[slot, 8 * t : 8 * t + 8, :] = value
        pick = bit(4)
        for t in range(size + 1):
            end = min(8, bins + 4 - 8 * t)
            v_ref[slot, 8 * t : 8 * t + end, :] = jnp.where(
                pick[:end], u_ref[slot, 8 * t + 4 : 8 * t + 4 + end, :], u_ref[slot, 8 * t : 8 * t + end, :]
            )
        pick = bit(2)
        for t in range(size + 1):
            end = min(8, bins + 2 - 8 * t)
            u_ref[slot, 8 * t : 8 * t + end, :] = jnp.where(
                pick[:end], v_ref[slot, 8 * t + 2 : 8 * t + 2 + end, :], v_ref[slot, 8 * t : 8 * t + end, :]
            )
        pick = bit(1)
        return [
            jnp.where(pick, u_ref[slot, 8 * t + 1 : 8 * t + 9, :], u_ref[slot, 8 * t : 8 * t + 8, :])
            for t in range(size)
        ]

    tiles = offset_ref.shape[1] // LANES
    build(0)
    for seg in range(2):
        if seg == 0:
            build(1)
        for tile in range(tiles):
            slot = seg * tiles + tile
            amp = jnp.dot(
                t_ref[seg], taps_ref[seg, :, tile * 2 * LANES : (tile + 1) * 2 * LANES],
                preferred_element_type=F32,
            )
            power = (amp * amp).reshape(blocks, 2, 16, 2 * LANES).sum(axis=1)
            power = power.reshape(span, 2 * LANES)
            p_ref[slot] = power[:, :LANES] + power[:, LANES:]
            for t, value in enumerate(moved(seg, tile, slot)):
                if seg == 0:
                    acc_ref[tile, 8 * t : 8 * t + 8, :] = value
                else:
                    acc_ref[tile, 8 * t : 8 * t + 8, :] += value
    each = LANES // out_ref.shape[1]
    for tile in range(tiles):
        turned = acc_ref[tile].T.astype(BF16)
        out_ref[tile * each : (tile + 1) * each] = turned.reshape(each, LANES // each, bins)


def total(scale, recv_ref, out_ref):
    value = recv_ref[0].astype(F32)
    for peer in range(1, recv_ref.shape[0]):
        value = value + recv_ref[peer].astype(F32)
    out_ref[...] = value * scale


def per_device(sft, doppler, antenna, coarse_index, freq_offset, wing_width):
    bins = sft.shape[3]
    peers = lax.axis_size("seg")
    count = lax.axis_size("band")
    templates = coarse_index.shape[1]
    fine = templates // peers
    segments = sft.shape[0] * peers
    tiles = templates // LANES
    span = bins + 2 * OMAX
    up = [(i, i + 1) for i in range(count - 1)]
    left = lax.ppermute(sft, "band", up)
    right = lax.ppermute(sft, "band", [(b, a) for a, b in up])
    taps = pl.pallas_call(
        make_taps,
        out_shape=jax.ShapeDtypeStruct((2, 4 * TAPS, 2 * templates), BF16),
        name="make_taps",
    )(doppler, antenna, coarse_index)
    vmem = pl.BlockSpec(memory_space=VMEM)
    sent = pl.pallas_call(
        segment_sums,
        out_shape=jax.ShapeDtypeStruct((peers, fine, bins), BF16),
        in_specs=[pl.BlockSpec(memory_space=pltpu.SMEM)] + [vmem] * 5,
        scratch_shapes=[
            VMEM((2, bins // LANES + 2, 8, LANES), F32),
            VMEM((2, 2 * span, 2 * LANES), BF16),
            VMEM((2 * tiles, span, LANES), F32),
            VMEM((2 * tiles, bins + 8, LANES), F32),
            VMEM((2 * tiles, bins + 8, LANES), F32),
            VMEM((tiles, bins, LANES), F32),
        ],
        name="segment_sums",
    )(wing_width, freq_offset, left, sft, right, taps)
    recv = lax.all_to_all(sent, "seg", 0, 0, tiled=True)
    return pl.pallas_call(
        lambda *refs: total(1.0 / (4 * segments), *refs),
        out_shape=jax.ShapeDtypeStruct((fine, bins), F32),
        name="total",
    )(recv)


def solution(mesh):
    placed = (
        P("seg", None, None, "band"),
        P("seg", None),
        P("seg", None, None, None),
        P("seg", None),
        P("seg", None),
        P(),
    )
    return jax.shard_map(
        per_device, mesh=mesh, in_specs=placed, out_specs=P("seg", "band"), check_vma=False
    )
```

time: 2200 us -> 40 us (0.02)
  the two profiles are of different devices: /device:TPU:27 before, /device:TPU:199 now
where the time goes in v2:
time: 40 us; the launch traced here: 39.6 us
  blocking collectives  20.9 us (52%)
  Pallas kernels  7.37 us (18%)
  starting transfers between devices  7.04 us (18%)
  waiting for transfers between devices  3.7 us (9%)
  local copies, waits for them, and re-layouts  0.59 us (1%)
    all_to_all x1, blocking collectives, per_device(): recv = lax.all_to_all(sent, 'seg', 0, 0, tiled=True)  20.9 us
    ppermute x1, starting transfers between devices, per_device(): left = lax.ppermute(sft, 'band', up)  5.12 us
    ppermute x1, waiting for transfers between devices, per_device(): right = lax.ppermute(sft, 'band', [(b, a) for a, b in up])  3.7 us
    pallas_call x1, Pallas kernels, per_device(): pl.pallas_call(segment_sums, out_shape=jax.ShapeDtypeStruct((peers, fine,...  3.51 us
    pallas_call x1, Pallas kernels, per_device(): pl.pallas_call(make_taps, out_shape=jax.ShapeDtypeStruct((2, 4 * TAPS, 2...  2.25 us
    ppermute x1, starting transfers between devices, per_device(): right = lax.ppermute(sft, 'band', [(b, a) for a, b in up])  1.92 us
    pallas_call x1, Pallas kernels, per_device(): pl.pallas_call(lambda *refs: total(1.0 / (4 * segments), *refs), out_shap...  1.61 us
  transfers between devices with their start and end apart: 2, of which 1 were waited for; matrix products, arithmetic and copies ran while one was open for 0% of the time, Pallas kernels for 6%

profile of v2, /device:TPU:199, one launch (start us, length us, event | category | flops | bytes accessed | tf_op | source)
XLA Modules:
  0.0 39.6 jit_solution(430700071306108239)
XLA Ops:
  0.0 5.1 %collective-permute-start = (bf16[2,2,2,256]{3,2,1,0:T(2,128)(2,1)}, bf16[2,2,2,256]{3,2,1,0:T(2,128)(2,1)S(1)}, u32[]{:S(2)}, u32[]{:S(2)}) collective-permute-start(bf16[2,2,2,256]{3,2,1,0:T(2,128)(2,1)} %own_ref.1), channel_id=1, source_target_pairs={{0,1},{1,2},{2,3},{3,4},{4,5},{5,6},{6,7},{7,8},{8,9},{9,10},{10,1... | collective-permute-start | bytes 12296 | tf_op jit(solution)/shard_map/ppermute | solution.py:211
  5.1 1.9 %collective-permute-start.1 = (bf16[2,2,2,256]{3,2,1,0:T(2,128)(2,1)}, bf16[2,2,2,256]{3,2,1,0:T(2,128)(2,1)S(1)}, u32[]{:S(2)}, u32[]{:S(2)}) collective-permute-start(bf16[2,2,2,256]{3,2,1,0:T(2,128)(2,1)} %own_ref.1), channel_id=1, source_target_pairs={{1,0},{2,1},{3,2},{4,3},{5,4},{6,5},{7,6},{8,7},{9,8},{10,9},{11,1... | collective-permute-start | bytes 12296 | tf_op jit(solution)/shard_map/ppermute | solution.py:212
  7.1 2.3 %make_taps.1.taps_ref = bf16[2,256,1024]{2,1,0:T(8,128)(2,1)} custom-call(f32[2,512]{1,0:T(2,128)} %doppler_ref.1, f32[2,2,2,512]{3,2,1,0:T(2,128)} %antenna_ref.1, s32[2,512]{1,0:T(2,128)} %index_ref.1), custom_call_target="tpu_custom_call" | custom-call | tf_op jit(solution)/shard_map/make_taps/pallas_call | solution.py:213
  9.3 0.0 collective-permute-done.left_ref
  9.3 0.0 copy-start
  9.3 3.7 %collective-permute-done.1.right_ref = bf16[2,2,2,256]{3,2,1,0:T(2,128)(2,1)S(1)} collective-permute-done((bf16[2,2,2,256]{3,2,1,0:T(2,128)(2,1)}, bf16[2,2,2,256]{3,2,1,0:T(2,128)(2,1)S(1)}, u32[]{:S(2)}, u32[]{:S(2)}) %collective-permute-start.1) | collective-permute-done | bytes 4128 | tf_op jit(solution)/shard_map/ppermute | solution.py:212
  13.0 0.0 copy-done
  13.0 0.0 copy-start.1
  13.0 0.6 %copy-done.1 = bf16[2,2,2,256]{3,2,1,0:T(2,128)(2,1)} copy-done((bf16[2,2,2,256]{3,2,1,0:T(2,128)(2,1)}, bf16[2,2,2,256]{3,2,1,0:T(2,128)(2,1)S(1)}, u32[]{:S(2)}) %copy-start.1) | copy-done | bytes 4120
  13.6 3.5 %segment_sums.1 = bf16[16,32,256]{2,1,0:T(8,128)(2,1)} custom-call(s32[32]{0:T(128)} %wing_ref.1, s32[2,512]{1,0:T(2,128)} %offset_ref.1, bf16[2,2,2,256]{3,2,1,0:T(2,128)(2,1)} %copy-done, bf16[2,2,2,256]{3,2,1,0:T(2,128)(2,1)} %own_ref.1, bf16[2,2,2,256]{3,2,1,0:T(2,128)(2,1)} %copy-done.1, bf16[2,256,1024]{2,1,0:T(8,128)(2,1)} %make_taps.1.taps_ref), custom_call_target="tpu_custom_call" | custom-call | tf_op jit(solution)/shard_map/segment_sums/pallas_call | solution.py:219
  17.1 20.9 %all_to_all.5.refs_0_ = bf16[16,32,256]{2,1,0:T(8,128)(2,1)} all-to-all(bf16[16,32,256]{2,1,0:T(8,128)(2,1)} %segment_sums.1), channel_id=1, replica_groups=mesh['seg'=16,'band'=32] {'seg'}, dimensions={0} | all-to-all | bytes 524288 | tf_op jit(solution)/shard_map/all_to_all | solution.py:233
  38.0 1.6 %total.1 = f32[32,256]{1,0:T(8,128)} custom-call(bf16[16,32,256]{2,1,0:T(8,128)(2,1)} %all_to_all.5.refs_0_), custom_call_target="tpu_custom_call" | custom-call | tf_op jit(solution)/shard_map/total/pallas_call | solution.py:234
Async XLA Ops:
  0.0 9.3 %collective-permute-start = (bf16[2,2,2,256]{3,2,1,0:T(2,128)(2,1)}, bf16[2,2,2,256]{3,2,1,0:T(2,128)(2,1)S(1)}, u32[]{:S(2)}, u32[]{:S(2)}) collective-permute-start(bf16[2,2,2,256]{3,2,1,0:T(2,128)(2,1)} %own_ref.1), channel_id=1, source_target_pairs={{0,1},{1,2},{2,3},{3,4},{4,5},{5,6},{6,7},{7,8},{8,9},{9,10},{10,1... | collective-permute-start | bytes 12296 | tf_op jit(solution)/shard_map/ppermute | solution.py:211
  5.1 7.9 %collective-permute-start.1 = (bf16[2,2,2,256]{3,2,1,0:T(2,128)(2,1)}, bf16[2,2,2,256]{3,2,1,0:T(2,128)(2,1)S(1)}, u32[]{:S(2)}, u32[]{:S(2)}) collective-permute-start(bf16[2,2,2,256]{3,2,1,0:T(2,128)(2,1)} %own_ref.1), channel_id=1, source_target_pairs={{1,0},{2,1},{3,2},{4,3},{5,4},{6,5},{7,6},{8,7},{9,8},{10,9},{11,1... | collective-permute-start | bytes 12296 | tf_op jit(solution)/shard_map/ppermute | solution.py:212
  9.3 3.7 %copy-start = (bf16[2,2,2,256]{3,2,1,0:T(2,128)(2,1)}, bf16[2,2,2,256]{3,2,1,0:T(2,128)(2,1)S(1)}, u32[]{:S(2)}) copy-start(bf16[2,2,2,256]{3,2,1,0:T(2,128)(2,1)S(1)} %collective-permute-done.left_ref) | copy-start | bytes 12292
  13.0 0.6 %copy-start.1 = (bf16[2,2,2,256]{3,2,1,0:T(2,128)(2,1)}, bf16[2,2,2,256]{3,2,1,0:T(2,128)(2,1)S(1)}, u32[]{:S(2)}) copy-start(bf16[2,2,2,256]{3,2,1,0:T(2,128)(2,1)S(1)} %collective-permute-done.1.right_ref) | copy-start | bytes 12292

commit v3 on v2

--- a/solution.py
+++ b/solution.py
@@ -1,3 +1,4 @@
+import functools
 import math
 
 import jax
@@ -40,6 +41,10 @@
     for n in reversed(range(8)):
         total = total * r2 + (-1) ** n * math.pi ** (2 * n) / math.factorial(2 * n + 1)
     return total * r
+
+
+def near(value):
+    return pltpu.with_memory_space_constraint(value, VMEM)
 
 
 def make_taps(doppler_ref, antenna_ref, index_ref, out_ref):
@@ -72,7 +77,7 @@
 
 
 def segment_sums(
-    wing_ref, offset_ref, left_ref, own_ref, right_ref, taps_ref, out_ref,
+    scale, wing_ref, offset_ref, left_ref, own_ref, right_ref, taps_ref, out_ref,
     chunk_ref, t_ref, p_ref, u_ref, v_ref, acc_ref
 ):
     bins = own_ref.shape[3]
@@ -187,15 +192,8 @@
                     acc_ref[tile, 8 * t : 8 * t + 8, :] += value
     each = LANES // out_ref.shape[1]
     for tile in range(tiles):
-        turned = acc_ref[tile].T.astype(BF16)
+        turned = (acc_ref[tile] * scale).T.astype(BF16)
         out_ref[tile * each : (tile + 1) * each] = turned.reshape(each, LANES // each, bins)
-
-
-def total(scale, recv_ref, out_ref):
-    value = recv_ref[0].astype(F32)
-    for peer in range(1, recv_ref.shape[0]):
-        value = value + recv_ref[peer].astype(F32)
-    out_ref[...] = value * scale
 
 
 def per_device(sft, doppler, antenna, coarse_index, freq_offset, wing_width):
@@ -212,13 +210,13 @@
     right = lax.ppermute(sft, "band", [(b, a) for a, b in up])
     taps = pl.pallas_call(
         make_taps,
-        out_shape=jax.ShapeDtypeStruct((2, 4 * TAPS, 2 * templates), BF16),
+        out_shape=VMEM((2, 4 * TAPS, 2 * templates), BF16),
         name="make_taps",
-    )(doppler, antenna, coarse_index)
+    )(near(doppler), near(antenna), near(coarse_index))
     vmem = pl.BlockSpec(memory_space=VMEM)
     sent = pl.pallas_call(
-        segment_sums,
-        out_shape=jax.ShapeDtypeStruct((peers, fine, bins), BF16),
+        functools.partial(segment_sums, 1.0 / (4 * segments)),
+        out_shape=VMEM((peers, fine, bins), BF16),
         in_specs=[pl.BlockSpec(memory_space=pltpu.SMEM)] + [vmem] * 5,
         scratch_shapes=[
             VMEM((2, bins // LANES + 2, 8, LANES), F32),
@@ -229,13 +227,9 @@
             VMEM((tiles, bins, LANES), F32),
         ],
         name="segment_sums",
-    )(wing_width, freq_offset, left, sft, right, taps)
+    )(wing_width, *[near(z) for z in (freq_offset, left, sft, right, taps)])
     recv = lax.all_to_all(sent, "seg", 0, 0, tiled=True)
-    return pl.pallas_call(
-        lambda *refs: total(1.0 / (4 * segments), *refs),
-        out_shape=jax.ShapeDtypeStruct((fine, bins), F32),
-        name="total",
-    )(recv)
+    return jnp.sum(recv.astype(F32), 0)
 
 
 def solution(mesh):

time: 40 us -> 36.9 us (0.922)
  Pallas kernels: 7.37 us -> 2.76 us
  local copies, waits for them, and re-layouts: 0.59 us -> 2.09 us
  other arithmetic: 0 us -> 0.66 us
  waiting for transfers between devices: 3.7 us -> 3.28 us
    pallas_call x3 -> x2, Pallas kernels: 7.37 us -> 2.76 us  [the longest x1 2.2 us: per_device(): pl.pallas_call(functools.partial(segment_sums, 1.0 / (4 * segments)), out...]
    unnamed x4 -> x10, local copies, waits for them, and re-layouts: 0.59 us -> 2.09 us
    reduce_sum x0 -> x1, other arithmetic: none -> 0.66 us  [per_device(): return jnp.sum(recv.astype(F32), 0)]
    ppermute x1, waiting for transfers between devices: 3.7 us -> 3.28 us  [per_device(): right = lax.ppermute(sft, 'band', [(b, a) for a, b in up])]
  transfers between devices with their start and end apart: 2 -> 2, of which waited for: 1 -> 1; matrix products, arithmetic and copies ran while one was open for 0% -> 0% of each run, Pallas kernels for 6% -> 2%
where the time goes in v3:
time: 36.9 us; the launch traced here: 36.5 us
  blocking collectives  20.6 us (56%)
  starting transfers between devices  7.03 us (19%)
  waiting for transfers between devices  3.28 us (9%)
  Pallas kernels  2.76 us (7%)
  local copies, waits for them, and re-layouts  2.09 us (6%)
  other arithmetic  0.66 us (2%)
    all_to_all x1, blocking collectives, per_device(): recv = lax.all_to_all(sent, 'seg', 0, 0, tiled=True)  20.6 us
    ppermute x1, starting transfers between devices, per_device(): left = lax.ppermute(sft, 'band', up)  5.11 us
    ppermute x1, waiting for transfers between devices, per_device(): right = lax.ppermute(sft, 'band', [(b, a) for a, b in up])  3.28 us
    pallas_call x1, Pallas kernels, per_device(): pl.pallas_call(functools.partial(segment_sums, 1.0 / (4 * segments)), out...  2.2 us
    unnamed x10, local copies, waits for them, and re-layouts  2.09 us
    ppermute x1, starting transfers between devices, per_device(): right = lax.ppermute(sft, 'band', [(b, a) for a, b in up])  1.92 us
  transfers between devices with their start and end apart: 2, of which 1 were waited for; matrix products, arithmetic and copies ran while one was open for 0% of the time, Pallas kernels for 2%

profile of v3, /device:TPU:199, one launch (start us, length us, event | category | flops | bytes accessed | tf_op | source)
XLA Modules:
  0.0 36.5 jit_solution(5030688818076887179)
XLA Ops:
  0.0 5.1 %collective-permute-start = (bf16[2,2,2,256]{3,2,1,0:T(2,128)(2,1)}, bf16[2,2,2,256]{3,2,1,0:T(2,128)(2,1)S(1)}, u32[]{:S(2)}, u32[]{:S(2)}) collective-permute-start(bf16[2,2,2,256]{3,2,1,0:T(2,128)(2,1)} %own_ref.1), channel_id=1, source_target_pairs={{0,1},{1,2},{2,3},{3,4},{4,5},{5,6},{6,7},{7,8},{8,9},{9,10},{10,1... | collective-permute-start | bytes 12296 | tf_op jit(solution)/shard_map/ppermute | solution.py:209
  5.1 1.9 %collective-permute-start.1 = (bf16[2,2,2,256]{3,2,1,0:T(2,128)(2,1)}, bf16[2,2,2,256]{3,2,1,0:T(2,128)(2,1)S(1)}, u32[]{:S(2)}, u32[]{:S(2)}) collective-permute-start(bf16[2,2,2,256]{3,2,1,0:T(2,128)(2,1)} %own_ref.1), channel_id=1, source_target_pairs={{1,0},{2,1},{3,2},{4,3},{5,4},{6,5},{7,6},{8,7},{9,8},{10,9},{11,1... | collective-permute-start | bytes 12296 | tf_op jit(solution)/shard_map/ppermute | solution.py:210
  7.0 0.0 copy-start
  7.1 0.7 %copy-done = f32[2,2,2,512]{3,2,1,0:T(2,128)S(1)} copy-done((f32[2,2,2,512]{3,2,1,0:T(2,128)S(1)}, f32[2,2,2,512]{3,2,1,0:T(2,128)}, u32[]{:S(2)}) %copy-start) | copy-done | bytes 16408
  7.8 0.0 copy-start.1
  7.8 0.7 %copy-done.1 = f32[2,512]{1,0:T(2,128)S(1)} copy-done((f32[2,512]{1,0:T(2,128)S(1)}, f32[2,512]{1,0:T(2,128)}, u32[]{:S(2)}) %copy-start.1) | copy-done | bytes 4120
  8.5 0.0 copy-start.2
  8.5 0.7 %copy-done.2 = s32[2,512]{1,0:T(2,128)S(1)} copy-done((s32[2,512]{1,0:T(2,128)S(1)}, s32[2,512]{1,0:T(2,128)}, u32[]{:S(2)}) %copy-start.2) | copy-done | bytes 4120
  9.1 0.0 copy-start.3
  9.1 0.0 copy-start.4
  9.1 0.6 %make_taps.1.taps_ref = bf16[2,256,1024]{2,1,0:T(8,128)(2,1)S(1)} custom-call(f32[2,512]{1,0:T(2,128)S(1)} %copy-done.1, f32[2,2,2,512]{3,2,1,0:T(2,128)S(1)} %copy-done, s32[2,512]{1,0:T(2,128)S(1)} %copy-done.2), custom_call_target="tpu_custom_call" | custom-call | tf_op jit(solution)/shard_map/make_taps/pallas_call | solution.py:211
  9.7 0.0 collective-permute-done.left_ref
  9.7 3.3 %collective-permute-done.1.right_ref = bf16[2,2,2,256]{3,2,1,0:T(2,128)(2,1)S(1)} collective-permute-done((bf16[2,2,2,256]{3,2,1,0:T(2,128)(2,1)}, bf16[2,2,2,256]{3,2,1,0:T(2,128)(2,1)S(1)}, u32[]{:S(2)}, u32[]{:S(2)}) %collective-permute-start.1) | collective-permute-done | bytes 4128 | tf_op jit(solution)/shard_map/ppermute | solution.py:210
  13.0 0.0 copy-done.3
  13.0 0.0 copy-done.4
  13.0 2.2 %segment_sums.1 = bf16[16,32,256]{2,1,0:T(8,128)(2,1)S(1)} custom-call(s32[32]{0:T(128)} %wing_ref.1, s32[2,512]{1,0:T(2,128)S(1)} %copy-done.3, bf16[2,2,2,256]{3,2,1,0:T(2,128)(2,1)S(1)} %collective-permute-done.left_ref, bf16[2,2,2,256]{3,2,1,0:T(2,128)(2,1)S(1)} %copy-done.4, bf16[2,2,2,256]{3,2,1,0:T(2,128)(2,1)S(1)} %collective-permute-done.1.right_ref, ...), custom_call_target="tpu_custom_call" | custom-call | tf_op jit(solution)/shard_map/segment_sums/pallas_call | solution.py:217
  15.2 20.6 %all_to_all.5 = bf16[16,32,256]{2,1,0:T(8,128)(2,1)S(1)} all-to-all(bf16[16,32,256]{2,1,0:T(8,128)(2,1)S(1)} %segment_sums.1), channel_id=1, replica_groups=mesh['seg'=16,'band'=32] {'seg'}, dimensions={0} | all-to-all | bytes 524288 | tf_op jit(solution)/shard_map/all_to_all | solution.py:231
  35.8 0.7 %convert_reduce_fusion = f32[32,256]{1,0:T(8,128)} fusion(bf16[16,32,256]{2,1,0:T(8,128)(2,1)S(1)} %all_to_all.5), kind=kLoop, calls=%fused_computation | loop fusion | flops 253952 | bytes 294912 | tf_op jit(solution)/shard_map/reduce_sum | solution.py:232
Async XLA Ops:
  0.0 9.7 %collective-permute-start = (bf16[2,2,2,256]{3,2,1,0:T(2,128)(2,1)}, bf16[2,2,2,256]{3,2,1,0:T(2,128)(2,1)S(1)}, u32[]{:S(2)}, u32[]{:S(2)}) collective-permute-start(bf16[2,2,2,256]{3,2,1,0:T(2,128)(2,1)} %own_ref.1), channel_id=1, source_target_pairs={{0,1},{1,2},{2,3},{3,4},{4,5},{5,6},{6,7},{7,8},{8,9},{9,10},{10,1... | collective-permute-start | bytes 12296 | tf_op jit(solution)/shard_map/ppermute | solution.py:209
  5.1 7.9 %collective-permute-start.1 = (bf16[2,2,2,256]{3,2,1,0:T(2,128)(2,1)}, bf16[2,2,2,256]{3,2,1,0:T(2,128)(2,1)S(1)}, u32[]{:S(2)}, u32[]{:S(2)}) collective-permute-start(bf16[2,2,2,256]{3,2,1,0:T(2,128)(2,1)} %own_ref.1), channel_id=1, source_target_pairs={{1,0},{2,1},{3,2},{4,3},{5,4},{6,5},{7,6},{8,7},{9,8},{10,9},{11,1... | collective-permute-start | bytes 12296 | tf_op jit(solution)/shard_map/ppermute | solution.py:210
  7.0 0.7 %copy-start = (f32[2,2,2,512]{3,2,1,0:T(2,128)S(1)}, f32[2,2,2,512]{3,2,1,0:T(2,128)}, u32[]{:S(2)}) copy-start(f32[2,2,2,512]{3,2,1,0:T(2,128)} %antenna_ref.1) | copy-start | bytes 49156
  7.8 0.7 %copy-start.1 = (f32[2,512]{1,0:T(2,128)S(1)}, f32[2,512]{1,0:T(2,128)}, u32[]{:S(2)}) copy-start(f32[2,512]{1,0:T(2,128)} %doppler_ref.1) | copy-start | bytes 12292
  8.5 0.7 %copy-start.2 = (s32[2,512]{1,0:T(2,128)S(1)}, s32[2,512]{1,0:T(2,128)}, u32[]{:S(2)}) copy-start(s32[2,512]{1,0:T(2,128)} %index_ref.1) | copy-start | bytes 12292
  9.1 3.9 %copy-start.3 = (s32[2,512]{1,0:T(2,128)S(1)}, s32[2,512]{1,0:T(2,128)}, u32[]{:S(2)}) copy-start(s32[2,512]{1,0:T(2,128)} %offset_ref.1) | copy-start | bytes 12292
  9.1 3.9 %copy-start.4 = (bf16[2,2,2,256]{3,2,1,0:T(2,128)(2,1)S(1)}, bf16[2,2,2,256]{3,2,1,0:T(2,128)(2,1)}, u32[]{:S(2)}) copy-start(bf16[2,2,2,256]{3,2,1,0:T(2,128)(2,1)} %own_ref.1) | copy-start | bytes 12292

commit v4 on v3

v4 whole, which is shorter than its diff:
```python
import functools
import math

import jax
import jax.numpy as jnp
from jax import lax
from jax.experimental import pallas as pl
from jax.experimental.pallas import tpu as pltpu
from jax.sharding import PartitionSpec as P

WMAX = 32
OMAX = 32
LANES = 128
TAPS = 2 * WMAX
HALF = LANES // 2
VMEM = pltpu.VMEM
F32 = jnp.float32
BF16 = jnp.bfloat16
INDEX_ROW = 5
OFFSET_ROW = 6
BIN_ROW = 16
PACKED_ROWS = 24


def lane_iota(shape):
    return lax.broadcasted_iota(jnp.int32, shape, len(shape) - 1)


def row_iota(shape):
    return lax.broadcasted_iota(jnp.int32, shape, len(shape) - 2)


def near(value):
    return pltpu.with_memory_space_constraint(value, VMEM)


def split(value, count):
    parts = []
    for _ in range(count):
        part = value.astype(BF16)
        parts.append(part)
        value = value - part.astype(F32)
    return parts


def sin_cos_pi(r):
    r2 = r * r
    sine = jnp.zeros_like(r)
    cosine = jnp.zeros_like(r)
    for n in reversed(range(9)):
        sine = sine * r2 + (-1) ** n * math.pi ** (2 * n + 1) / math.factorial(2 * n + 1)
        cosine = cosine * r2 + (-1) ** n * math.pi ** (2 * n) / math.factorial(2 * n)
    return sine * r, cosine


def pack(sft_ref, doppler_ref, antenna_ref, index_ref, offset_ref, out_ref):
    bins = sft_ref.shape[3]
    out_ref[...] = jnp.zeros_like(out_ref)
    for s in range(2):
        out_ref[8 * s : 8 * s + 1, :] = doppler_ref[s : s + 1, :]
        for q in range(2):
            out_ref[8 * s + 1 + 2 * q : 8 * s + 3 + 2 * q, :] = antenna_ref[s, q]
        at = 8 * s + INDEX_ROW
        out_ref[at : at + 1, :] = index_ref[s : s + 1, :].astype(F32)
        at = 8 * s + OFFSET_ROW
        out_ref[at : at + 1, :] = offset_ref[s : s + 1, :].astype(F32)
        for d in range(2):
            at = BIN_ROW + 4 * s + 2 * d
            out_ref[at : at + 2, :bins] = sft_ref[s, d].astype(F32)


def make_taps(wing_ref, packed_ref, out_ref, reach_ref):
    band = lax.axis_index("band")
    last = lax.axis_size("band") - 1
    core = lax.rem(lax.axis_index("seg"), 2)
    beside = jnp.where(core == 0, band - 1, band + 1)
    w_own = wing_ref[band]
    w_beside = wing_ref[jnp.clip(beside, 0, last)]
    w_beside = jnp.where((beside < 0) | (beside > last), 0, w_beside)
    row = row_iota(reach_ref.shape)
    reach = jnp.where((row == 0) & (core == 0) | (row == 2) & (core == 1), w_beside, w_own)
    reach_ref[...] = reach.astype(F32)

    templates = packed_ref.shape[2]
    tap = (WMAX - 1) - row_iota((TAPS, LANES)).astype(F32)
    for seg in range(4):
        side, s = divmod(seg, 2)
        values = packed_ref[side, 8 * s : 8 * s + 5, :]
        table = jnp.concatenate(
            [part.astype(F32) for part in split(values, 3)] + [jnp.zeros((1, templates), F32)], 0
        ).astype(BF16)
        at = 8 * s + INDEX_ROW
        index = packed_ref[side, at : at + 1, :].astype(jnp.int32)
        for tile in range(templates // LANES):
            cols = slice(tile * LANES, (tile + 1) * LANES)
            hot = row_iota((templates, LANES)) == index[:, cols]
            chosen = jnp.dot(table, jnp.where(hot, 1.0, 0.0).astype(BF16), preferred_element_type=F32)
            whole = chosen[0:5] + chosen[5:10] + chosen[10:15]
            shift = whole[0:1]
            sine, cosine = sin_cos_pi(shift - jnp.round(shift))
            factor = sine * (-1.0 / math.pi)
            u = tap - shift
            whole_bin = u == 0
            inverse = 1.0 / u
            real = jnp.where(whole_bin, 1.0, factor * cosine * inverse)
            imag = jnp.where(whole_bin, 0.0, factor * sine * inverse)
            for q in range(2):
                at = (tile * 2 + q) * LANES
                for d in range(2):
                    weight = whole[1 + q * 2 + d : 2 + q * 2 + d]
                    for part, value in enumerate((real, imag)):
                        top = (2 * part + d) * TAPS
                        out_ref[seg, top : top + TAPS, at : at + LANES] = (weight * value).astype(BF16)


def segment_sums(
    scale, packed_ref, halo_ref, reach_ref, taps_ref, out_ref,
    chunk_ref, t_ref, p_ref, u_ref, v_ref, acc_ref
):
    bins = out_ref.shape[2]
    span = bins + 2 * OMAX
    blocks = span // 16
    segs = taps_ref.shape[0]
    core = lax.rem(lax.axis_index("seg"), 2)

    mirror = jnp.where(
        row_iota((LANES, LANES)) + lane_iota((LANES, LANES)) == LANES - 1, 1.0, 0.0
    ).astype(BF16)
    own = [
        jnp.concatenate(
            [packed_ref[side, BIN_ROW:PACKED_ROWS, c * LANES : (c + 1) * LANES] for side in range(2)], 0
        )
        for c in range(2)
    ]
    halo = [
        jnp.concatenate(
            [halo_ref[side, :, c * LANES : (c + 1) * LANES].astype(F32) for side in range(2)], 0
        )
        for c in range(2)
    ]
    first = core == 0
    parts = [
        jnp.where(first, own[1], halo[0]),
        jnp.where(first, own[0], own[1]),
        jnp.where(first, halo[1], own[0]),
    ]
    flipped = jnp.dot(
        jnp.concatenate(parts, 0).astype(BF16), mirror, preferred_element_type=F32
    )
    swapped = pltpu.roll(flipped, HALF, 1)
    for i in range(3):
        chunk_ref[0, i] = flipped[16 * i : 16 * i + 16]
        chunk_ref[1, i] = swapped[16 * i : 16 * i + 16]

    low_half = lane_iota((16, LANES)) < HALF
    within = lane_iota((16, LANES)) % HALF
    bend = within - row_iota((16, LANES))
    center = jnp.abs((WMAX - 0.5) - within.astype(F32))
    reach = [center < reach_ref[i : i + 1, :] for i in range(3)]

    def half_row(h, place, row):
        chunk, half = (h + 1) // 2, (h + 1) % 2
        return jnp.broadcast_to(chunk_ref[half ^ place, chunk, row : row + 1, :], (16, LANES))

    def build(seg):
        for ri in range(2):
            det0, det1 = seg * 4 + ri, seg * 4 + 2 + ri
            for h in range(span // HALF):
                source = jnp.where(low_half, half_row(h, 0, det0), half_row(h, 1, det1))
                after = jnp.where(low_half, half_row(h + 1, 0, det1), half_row(h + 1, 1, det0))
                for a in range(1, 5):
                    turn = LANES - 16 * a
                    window = jnp.where(
                        bend < HALF - 16 * a,
                        pltpu.roll(source, turn, 1, stride=1, stride_axis=0),
                        pltpu.roll(after, turn, 1, stride=1, stride_axis=0),
                    )
                    block = blocks - 4 * h - a
                    side = 0 if block < OMAX // 16 else (2 if block >= blocks - OMAX // 16 else 1)
                    window = jnp.where(reach[side], window, 0.0)
                    same = slice(block * 32 + ri * 16, block * 32 + ri * 16 + 16)
                    other = slice(block * 32 + 16 - ri * 16, block * 32 + 32 - ri * 16)
                    t_ref[seg, same, :LANES] = window.astype(BF16)
                    t_ref[seg, other, LANES:] = (-window if ri else window).astype(BF16)

    def moved(seg, tile, slot):
        at = 8 * (seg % 2) + OFFSET_ROW
        amount = packed_ref[seg // 2, at : at + 1, tile * LANES : (tile + 1) * LANES]
        amount = amount.astype(jnp.int32) + OMAX
        bit = lambda b: jnp.broadcast_to((amount & b) != 0, (8, LANES))
        size = bins // 8
        tiles = [p_ref[slot, 8 * t : 8 * t + 8, :] for t in range(span // 8)]
        far = bit(64)
        tiles = [jnp.where(far, tiles[t + 8], tiles[t]) for t in range(size)] + tiles[size:]
        for b in (32, 16, 8):
            pick, step = bit(b), b // 8
            tiles = [jnp.where(pick, tiles[t + step], tiles[t]) for t in range(size + step)]
        for t, value in enumerate(tiles):
            u_ref[slot, 8 * t : 8 * t + 8, :] = value
        for b, from_ref, to_ref in ((4, u_ref, v_ref), (2, v_ref, u_ref)):
            pick = bit(b)
            for t in range(size + 1):
                end = min(8, bins + b - 8 * t)
                to_ref[slot, 8 * t : 8 * t + end, :] = jnp.where(
                    pick[:end],
                    from_ref[slot, 8 * t + b : 8 * t + b + end, :],
                    from_ref[slot, 8 * t : 8 * t + end, :],
                )
        pick = bit(1)
        return [
            jnp.where(pick, u_ref[slot, 8 * t + 1 : 8 * t + 9, :], u_ref[slot, 8 * t : 8 * t + 8, :])
            for t in range(size)
        ]

    tiles = taps_ref.shape[2] // (2 * LANES)
    each = LANES // out_ref.shape[1]
    build(0)
    for seg in range(segs):
        if seg + 1 < segs:
            build(seg + 1)
        for tile in range(tiles):
            slot = seg * tiles + tile
            amp = jnp.dot(
                t_ref[seg], taps_ref[seg, :, tile * 2 * LANES : (tile + 1) * 2 * LANES],
                preferred_element_type=F32,
            )
            power = (amp * amp).reshape(blocks, 2, 16, 2 * LANES).sum(axis=1)
            power = power.reshape(span, 2 * LANES)
            p_ref[slot] = power[:, :LANES] + power[:, LANES:]
            for t, value in enumerate(moved(seg, tile, slot)):
                if seg == 0:
                    acc_ref[tile, 8 * t : 8 * t + 8, :] = value
                else:
                    acc_ref[tile, 8 * t : 8 * t + 8, :] += value
            if seg == segs - 1:
                turned = (acc_ref[tile] * scale).T.astype(BF16)
                out_ref[tile * each : (tile + 1) * each] = turned.reshape(each, LANES // each, bins)


def per_device(sft, doppler, antenna, coarse_index, freq_offset, wing_width):
    bins = sft.shape[3]
    peers = lax.axis_size("seg")
    count = lax.axis_size("band")
    templates = coarse_index.shape[1]
    fine = templates // peers
    segments = sft.shape[0] * peers
    tiles = templates // LANES
    here = bins // 2
    span = here + 2 * OMAX
    packed = pl.pallas_call(
        pack, out_shape=VMEM((PACKED_ROWS, templates), F32), name="pack"
    )(sft, doppler, antenna, coarse_index, freq_offset)
    pairs = [[i, i + 1] for i in range(0, peers, 2)]
    packed = lax.all_gather(packed[None], "seg", axis=0, tiled=True, axis_index_groups=pairs)
    rows = packed[:, BIN_ROW:, :bins].astype(BF16)
    swap = []
    for low, high in pairs:
        for b in range(1, count):
            swap += [(low * count + b, high * count + b - 1), (high * count + b - 1, low * count + b)]
    halo = lax.ppermute(rows, ("seg", "band"), swap)
    taps, reach = pl.pallas_call(
        make_taps,
        out_shape=(VMEM((4, 4 * TAPS, 2 * templates), BF16), VMEM((8, LANES), F32)),
        in_specs=[pl.BlockSpec(memory_space=pltpu.SMEM), pl.BlockSpec(memory_space=VMEM)],
        name="make_taps",
    )(wing_width, near(packed))
    sent = pl.pallas_call(
        functools.partial(segment_sums, 1.0 / (4 * segments)),
        out_shape=VMEM((peers, fine, here), BF16),
        scratch_shapes=[
            VMEM((2, 3, 16, LANES), F32),
            VMEM((4, 2 * span, 2 * LANES), BF16),
            VMEM((4 * tiles, span, LANES), F32),
            VMEM((4 * tiles, here + 8, LANES), F32),
            VMEM((4 * tiles, here + 8, LANES), F32),
            VMEM((tiles, here, LANES), F32),
        ],
        name="segment_sums",
    )(*[near(z) for z in (packed, halo, reach, taps)])
    recv = lax.all_to_all(sent, "seg", 0, 0, tiled=True)
    halves = jnp.sum(recv.astype(F32).reshape(peers // 2, 2, fine, here), 0)
    return jnp.concatenate([halves[0], halves[1]], 1)


def solution(mesh):
    placed = (
        P("seg", None, None, "band"),
        P("seg", None),
        P("seg", None, None, None),
        P("seg", None),
        P("seg", None),
        P(),
    )
    return jax.shard_map(
        per_device, mesh=mesh, in_specs=placed, out_specs=P("seg", "band"), check_vma=False
    )
```

time: 36.9 us -> 30 us (0.81)
  the two profiles are of different devices: /device:TPU:199 before, /device:TPU:257 now
where the time goes in v4:
time: 30 us; the launch traced here: 29.8 us
  blocking collectives  21.5 us (72%)
  Pallas kernels  4.25 us (14%)
  starting transfers between devices  3.35 us (11%)
  other arithmetic  0.64 us (2%)
    all_to_all x1, blocking collectives, per_device(): recv = lax.all_to_all(sent, 'seg', 0, 0, tiled=True)  19.3 us
    ppermute x1, starting transfers between devices, per_device(): halo = lax.ppermute(rows, ('seg', 'band'), swap)  3.35 us
    all_gather x1, blocking collectives, per_device(): lax.all_gather(packed[None], 'seg', axis=0, tiled=True, axis_index_groups...  2.2 us
    pallas_call x1, Pallas kernels, per_device(): pl.pallas_call(make_taps, out_shape=(VMEM((4, 4 * TAPS, 2 * templates), B...  1.76 us
    pallas_call x1, Pallas kernels, per_device(): pl.pallas_call(functools.partial(segment_sums, 1.0 / (4 * segments)), out...  1.71 us
    pallas_call x1, Pallas kernels, per_device(): pl.pallas_call(pack, out_shape=VMEM((PACKED_ROWS, templates), F32), name=...  0.78 us
    concatenate x1, other arithmetic, per_device(): return jnp.concatenate([halves[0], halves[1]], 1)  0.62 us
  transfers between devices with their start and end apart: 1, of which 0 were waited for; matrix products, arithmetic and copies ran while one was open for 0% of the time, Pallas kernels for 6%

profile of v4, /device:TPU:257, one launch (start us, length us, event | category | flops | bytes accessed | tf_op | source)
XLA Modules:
  0.0 29.8 jit_solution(18255837521585659278)
XLA Ops:
  0.0 0.8 %pack.1 = f32[24,512]{1,0:T(8,128)S(1)} custom-call(bf16[2,2,2,256]{3,2,1,0:T(2,128)(2,1)} %sft_ref.1, f32[2,512]{1,0:T(2,128)} %doppler_ref.1, f32[2,2,2,512]{3,2,1,0:T(2,128)} %antenna_ref.1, s32[2,512]{1,0:T(2,128)} %index_ref.1, s32[2,512]{1,0:T(2,128)} %offset_ref.1), custom_call_target="tpu_custom_call" | custom-call | tf_op jit(solution)/shard_map/pack/pallas_call | solution.py:250
  0.8 2.2 %all-gather = f32[48,512]{1,0:T(8,128)S(1)} all-gather(f32[24,512]{1,0:T(8,128)S(1)} %pack.1), channel_id=2, replica_groups={{0,32},{64,96},{128,160},{192,224},{256,288},{320,352},{384,416},{448,4..., dimensions={0}, use_global_device_ids=true | all-gather | bytes 147456 | tf_op jit(solution)/shard_map/all_gather | solution.py:254
  3.0 3.3 %collective-permute-start = (bf16[2,8,256]{2,1,0:T(8,128)(2,1)S(1)}, bf16[2,8,256]{2,1,0:T(8,128)(2,1)S(1)}, u32[]{:S(2)}, u32[]{:S(2)}) collective-permute-start(bf16[2,8,256]{2,1,0:T(8,128)(2,1)S(1)} %slice.19), channel_id=1, source_target_pairs={{1,32},{32,1},{2,33},{33,2},{3,34},{34,3},{4,35},{35,4},{5,36},{36... | collective-permute-start | bytes 24584 | tf_op jit(solution)/shard_map/ppermute | solution.py:260
  6.3 1.8 %make_taps.1 = (bf16[4,256,1024]{2,1,0:T(8,128)(2,1)S(1)}, f32[8,128]{1,0:T(8,128)S(1)}) custom-call(s32[32]{0:T(128)} %wing_ref.1, f32[2,24,512]{2,1,0:T(8,128)S(1)} %bitcast.8), custom_call_target="tpu_custom_call" | custom-call | tf_op jit(solution)/shard_map/make_taps/pallas_call | solution.py:261
  8.1 0.0 collective-permute-done.halo_ref
  8.1 1.7 %segment_sums.1 = bf16[16,32,128]{2,1,0:T(8,128)(2,1)S(1)} custom-call(f32[2,24,512]{2,1,0:T(8,128)S(1)} %bitcast.9, bf16[2,8,256]{2,1,0:T(8,128)(2,1)S(1)} %collective-permute-done.halo_ref, f32[8,128]{1,0:T(8,128)S(1)} %get-tuple-element.7.reach_ref, bf16[4,256,1024]{2,1,0:T(8,128)(2,1)S(1)} %get-tuple-element.8.taps_ref), custom_call_target="tpu_custom_call" | custom-call | tf_op jit(solution)/shard_map/segment_sums/pallas_call | solution.py:267
  9.8 19.3 %all_to_all.5 = bf16[16,32,128]{2,1,0:T(8,128)(2,1)S(1)} all-to-all(bf16[16,32,128]{2,1,0:T(8,128)(2,1)S(1)} %segment_sums.1), channel_id=1, replica_groups=mesh['seg'=16,'band'=32] {'seg'}, dimensions={0} | all-to-all | bytes 262144 | tf_op jit(solution)/shard_map/all_to_all | solution.py:280
  29.2 0.6 %pad_maximum_fusion = f32[32,256]{1,0:T(8,128)} fusion(f32[32,128]{1,0:T(8,128)S(1)} %get-tuple-element.10, f32[32,128]{1,0:T(8,128)S(1)} %get-tuple-element.9), kind=kLoop, calls=%fused_computation.1 | loop fusion | flops 8192 | bytes 65536 | tf_op jit(solution)/shard_map/concatenate | solution.py:282
  (3 shorter events, 0.0 us)
Async XLA Ops:
  3.0 5.1 %collective-permute-start = (bf16[2,8,256]{2,1,0:T(8,128)(2,1)S(1)}, bf16[2,8,256]{2,1,0:T(8,128)(2,1)S(1)}, u32[]{:S(2)}, u32[]{:S(2)}) collective-permute-start(bf16[2,8,256]{2,1,0:T(8,128)(2,1)S(1)} %slice.19), channel_id=1, source_target_pairs={{1,32},{32,1},{2,33},{33,2},{3,34},{34,3},{4,35},{35,4},{5,36},{36... | collective-permute-start | bytes 24584 | tf_op jit(solution)/shard_map/ppermute | solution.py:260

commit v5 on v4

v5 whole, which is shorter than its diff:
```python
import functools
import math

import jax
import jax.numpy as jnp
from jax import lax
from jax.experimental import pallas as pl
from jax.experimental.pallas import tpu as pltpu
from jax.sharding import PartitionSpec as P

WMAX = 32
OMAX = 32
LANES = 128
TAPS = 2 * WMAX
HALF = LANES // 2
VMEM = pltpu.VMEM
F32 = jnp.float32
BF16 = jnp.bfloat16
INDEX_ROW = 5
OFFSET_ROW = 6
BIN_ROW = 16
PACKED_ROWS = 24


def lane_iota(shape):
    return lax.broadcasted_iota(jnp.int32, shape, len(shape) - 1)


def row_iota(shape):
    return lax.broadcasted_iota(jnp.int32, shape, len(shape) - 2)


def near(value):
    return pltpu.with_memory_space_constraint(value, VMEM)


def split(value, count):
    parts = []
    for _ in range(count):
        part = value.astype(BF16)
        parts.append(part)
        value = value - part.astype(F32)
    return parts


def sin_cos_pi(r):
    r2 = r * r
    sine = jnp.zeros_like(r)
    cosine = jnp.zeros_like(r)
    for n in reversed(range(9)):
        sine = sine * r2 + (-1) ** n * math.pi ** (2 * n + 1) / math.factorial(2 * n + 1)
        cosine = cosine * r2 + (-1) ** n * math.pi ** (2 * n) / math.factorial(2 * n)
    return sine * r, cosine


def pack(sft_ref, doppler_ref, antenna_ref, index_ref, offset_ref, out_ref):
    bins = sft_ref.shape[3]
    out_ref[...] = jnp.zeros_like(out_ref)
    for s in range(2):
        out_ref[8 * s : 8 * s + 1, :] = doppler_ref[s : s + 1, :]
        for q in range(2):
            out_ref[8 * s + 1 + 2 * q : 8 * s + 3 + 2 * q, :] = antenna_ref[s, q]
        at = 8 * s + INDEX_ROW
        out_ref[at : at + 1, :] = index_ref[s : s + 1, :].astype(F32)
        at = 8 * s + OFFSET_ROW
        out_ref[at : at + 1, :] = offset_ref[s : s + 1, :].astype(F32)
        for d in range(2):
            at = BIN_ROW + 4 * s + 2 * d
            out_ref[at : at + 2, :bins] = sft_ref[s, d].astype(F32)


def mirrored(parts):
    mirror = jnp.where(
        row_iota((LANES, LANES)) + lane_iota((LANES, LANES)) == LANES - 1, 1.0, 0.0
    ).astype(BF16)
    flipped = jnp.dot(jnp.concatenate(parts, 0).astype(BF16), mirror, preferred_element_type=F32)
    swapped = pltpu.roll(flipped, HALF, 1)
    count = parts[0].shape[0]
    cut = lambda value: [value[count * i : count * i + count] for i in range(len(parts))]
    return cut(flipped), cut(swapped)


def own_bins(packed_ref, chunk):
    return jnp.concatenate(
        [packed_ref[side, BIN_ROW:PACKED_ROWS, chunk * LANES : (chunk + 1) * LANES] for side in range(2)], 0
    )


def build_windows(t_ref, chunk_ref, seg, ri, index, last_block, reach):
    low_half = lane_iota((16, LANES)) < HALF
    bend = lane_iota((16, LANES)) % HALF - row_iota((16, LANES))

    def half_row(h, place, row):
        return jnp.broadcast_to(chunk_ref[place, h, row : row + 1, :], (16, LANES))

    det0, det1 = seg * 4 + ri, seg * 4 + 2 + ri
    source = jnp.where(low_half, half_row(index, 0, det0), half_row(index, 1, det1))
    after = jnp.where(low_half, half_row(index + 1, 0, det1), half_row(index + 1, 1, det0))
    for a in range(1, 5):
        turn = LANES - 16 * a
        window = jnp.where(
            bend < HALF - 16 * a,
            pltpu.roll(source, turn, 1, stride=1, stride_axis=0),
            pltpu.roll(after, turn, 1, stride=1, stride_axis=0),
        )
        block = last_block - a
        window = jnp.where(reach[block], window, 0.0)
        same = slice(block * 32 + ri * 16, block * 32 + ri * 16 + 16)
        other = slice(block * 32 + 16 - ri * 16, block * 32 + 32 - ri * 16)
        t_ref[seg, same, :LANES] = window.astype(BF16)
        t_ref[seg, other, LANES:] = (-window if ri else window).astype(BF16)


def power_of(rows, taps):
    amp = jnp.dot(rows, taps, preferred_element_type=F32)
    power = (amp * amp).reshape(rows.shape[0] // 32, 2, 16, 2 * LANES).sum(axis=1)
    power = power.reshape(rows.shape[0] // 2, 2 * LANES)
    return power[:, :LANES] + power[:, LANES:]


def tap_center():
    within = lane_iota((16, LANES)) % HALF
    return jnp.abs((WMAX - 0.5) - within.astype(F32))


def shifted(tiles, packed_ref, seg, tile, u_ref, v_ref):
    at = 8 * (seg % 2) + OFFSET_ROW
    amount = packed_ref[seg // 2, at : at + 1, tile * LANES : (tile + 1) * LANES]
    amount = amount.astype(jnp.int32) + OMAX
    bit = lambda b: jnp.broadcast_to((amount & b) != 0, (8, LANES))
    size = len(tiles) - 8
    rows = 8 * size
    far = bit(64)
    tiles = [jnp.where(far, tiles[t + 8], tiles[t]) for t in range(size)] + tiles[size:]
    for b in (32, 16, 8):
        pick, step = bit(b), b // 8
        tiles = [jnp.where(pick, tiles[t + step], tiles[t]) for t in range(size + step)]
    for t, value in enumerate(tiles):
        u_ref[8 * t : 8 * t + 8, :] = value
    for b, from_ref, to_ref in ((4, u_ref, v_ref), (2, v_ref, u_ref)):
        pick = bit(b)
        for t in range(size + 1):
            end = min(8, rows + b - 8 * t)
            to_ref[8 * t : 8 * t + end, :] = jnp.where(
                pick[:end], from_ref[8 * t + b : 8 * t + b + end, :], from_ref[8 * t : 8 * t + end, :]
            )
    pick = bit(1)
    return [
        jnp.where(pick, u_ref[8 * t + 1 : 8 * t + 9, :], u_ref[8 * t : 8 * t + 8, :])
        for t in range(size)
    ]


def add_tiles(total_ref, tile, values, start):
    for t, value in enumerate(values):
        if start:
            total_ref[tile, 8 * t : 8 * t + 8, :] = value
        else:
            total_ref[tile, 8 * t : 8 * t + 8, :] += value


def inner_power(
    wing_ref, packed_ref, taps_ref, reach_ref, middle_ref, total_ref,
    chunk_ref, t_ref, u_ref, v_ref
):
    band = lax.axis_index("band")
    last = lax.axis_size("band") - 1
    core = lax.rem(lax.axis_index("seg"), 2)
    first = core == 0
    beside = jnp.where(first, band - 1, band + 1)
    w_own = wing_ref[band]
    w_beside = wing_ref[jnp.clip(beside, 0, last)]
    w_beside = jnp.where((beside < 0) | (beside > last), 0, w_beside)
    row = row_iota(reach_ref.shape)
    reach = jnp.where((row == 0) & (core == 0) | (row == 2) & (core == 1), w_beside, w_own)
    reach_ref[...] = reach.astype(F32)

    templates = packed_ref.shape[2]
    tap = (WMAX - 1) - row_iota((TAPS, LANES)).astype(F32)
    for seg in range(4):
        side, s = divmod(seg, 2)
        values = packed_ref[side, 8 * s : 8 * s + 5, :]
        table = jnp.concatenate(
            [part.astype(F32) for part in split(values, 3)] + [jnp.zeros((1, templates), F32)], 0
        ).astype(BF16)
        groups = templates // LANES
        table = jnp.concatenate([table[:, g * LANES : (g + 1) * LANES] for g in range(groups)], 0)
        for tile in range(groups):
            at = 8 * s + INDEX_ROW
            index = packed_ref[side, at : at + 1, tile * LANES : (tile + 1) * LANES].astype(jnp.int32)
            group, place = index // LANES, index % LANES
            hot = jnp.where(row_iota((LANES, LANES)) == place, 1.0, 0.0).astype(BF16)
            found = jnp.dot(table, hot, preferred_element_type=F32)
            chosen = found[:16]
            for g in range(1, groups):
                chosen = jnp.where(group == g, found[16 * g : 16 * g + 16], chosen)
            whole = chosen[0:5] + chosen[5:10] + chosen[10:15]
            shift = whole[0:1]
            sine, cosine = sin_cos_pi(shift - jnp.round(shift))
            factor = sine * (-1.0 / math.pi)
            u = tap - shift
            whole_bin = u == 0
            inverse = 1.0 / u
            real = jnp.where(whole_bin, 1.0, factor * cosine * inverse)
            imag = jnp.where(whole_bin, 0.0, factor * sine * inverse)
            for q in range(2):
                at = (tile * 2 + q) * LANES
                for d in range(2):
                    weight = whole[1 + q * 2 + d : 2 + q * 2 + d]
                    for part, value in enumerate((real, imag)):
                        top = (2 * part + d) * TAPS
                        taps_ref[seg, top : top + TAPS, at : at + LANES] = (weight * value).astype(BF16)

    flipped, swapped = mirrored([own_bins(packed_ref, 1), own_bins(packed_ref, 0)])
    halves = (
        ((swapped[0], flipped[0]), (flipped[0], swapped[0])),
        ((flipped[1], swapped[1]), (swapped[0], flipped[0])),
        ((swapped[1], flipped[1]), (flipped[1], swapped[1])),
    )
    for i, (even, odd) in enumerate(halves):
        for place in range(2):
            chunk_ref[place, i] = jnp.where(first, even[place], odd[place])
    near_reach = [tap_center() < w_own.astype(F32)] * 8
    tiles = templates // LANES
    for seg in range(4):
        for ri in range(2):
            for i in range(2):
                build_windows(t_ref, chunk_ref, seg, ri, i, 8 - 4 * i, near_reach)
        for tile in range(tiles):
            slot = seg * tiles + tile
            power = power_of(
                t_ref[seg], taps_ref[seg, :, tile * 2 * LANES : (tile + 1) * 2 * LANES]
            )
            middle_ref[slot] = jnp.where(first, power[:HALF], power[HALF:])
            parts = [power[8 * t : 8 * t + 8] for t in range(LANES // 8)]
            values = shifted(parts, packed_ref, seg, tile, u_ref.at[slot], v_ref.at[slot])
            add_tiles(total_ref, tile, values, seg == 0)


def segment_sums(
    scale, packed_ref, halo_ref, reach_ref, taps_ref, middle_ref, total_ref, out_ref,
    chunk_ref, t_ref, u_ref, v_ref, acc_ref, *p_refs
):
    bins = out_ref.shape[2]
    segs = taps_ref.shape[0]
    first = lax.rem(lax.axis_index("seg"), 2) == 0
    halo = [
        jnp.concatenate(
            [halo_ref[side, :, c * LANES : (c + 1) * LANES].astype(F32) for side in range(2)], 0
        )
        for c in range(2)
    ]
    parts = [
        jnp.where(first, own_bins(packed_ref, 0), halo[0]),
        jnp.where(first, halo[1], own_bins(packed_ref, 1)),
    ]
    flipped, swapped = mirrored(parts)
    for i, (low, high) in enumerate(((swapped[0], flipped[0]), (flipped[1], swapped[1]))):
        chunk_ref[0, i] = low
        chunk_ref[1, i] = high
    center = tap_center()
    below, above = (center < reach_ref[i : i + 1, :] for i in (0, 2))
    edge_start = pl.multiple_of(jnp.where(first, 0, HALF), 8)
    middle_start = pl.multiple_of(jnp.where(first, HALF, 0), 8)

    tiles = taps_ref.shape[2] // (2 * LANES)
    each = LANES // out_ref.shape[1]
    for seg in range(segs):
        for ri in range(2):
            build_windows(t_ref, chunk_ref, seg, ri, 0, 4, [below, below, above, above])
    for seg in range(segs):
        for tile in range(tiles):
            slot = seg * tiles + tile
            p_refs[slot][pl.ds(middle_start, HALF), :] = middle_ref[slot]
            p_refs[slot][pl.ds(edge_start, HALF), :] = power_of(
                t_ref[seg], taps_ref[seg, :, tile * 2 * LANES : (tile + 1) * 2 * LANES]
            )
            parts = [p_refs[slot][8 * t : 8 * t + 8, :] for t in range(LANES // 8)]
            values = shifted(parts, packed_ref, seg, tile, u_ref.at[slot], v_ref.at[slot])
            add_tiles(acc_ref, tile, values, seg == 0)
            if seg == segs - 1:
                edge, inner = acc_ref[tile], total_ref[tile]
                whole = jnp.concatenate(
                    [jnp.where(first, edge, inner), jnp.where(first, inner, edge)], 0
                )
                turned = (whole * scale).T.astype(BF16)
                out_ref[tile * each : (tile + 1) * each] = turned.reshape(each, LANES // each, bins)


def per_device(sft, doppler, antenna, coarse_index, freq_offset, wing_width):
    bins = sft.shape[3]
    peers = lax.axis_size("seg")
    count = lax.axis_size("band")
    templates = coarse_index.shape[1]
    fine = templates // peers
    segments = sft.shape[0] * peers
    tiles = templates // LANES
    here = bins // 2
    packed = pl.pallas_call(
        pack, out_shape=VMEM((PACKED_ROWS, templates), F32), name="pack"
    )(sft, doppler, antenna, coarse_index, freq_offset)
    pairs = [[i, i + 1] for i in range(0, peers, 2)]
    packed = lax.all_gather(packed[None], "seg", axis=0, tiled=True, axis_index_groups=pairs)
    rows = packed[:, BIN_ROW:, :bins].astype(BF16)
    swap = []
    for low, high in pairs:
        for b in range(1, count):
            swap += [(low * count + b, high * count + b - 1), (high * count + b - 1, low * count + b)]
    halo = lax.ppermute(rows, ("seg", "band"), swap)
    slots = 4 * tiles
    taps, reach, middle, inner = pl.pallas_call(
        inner_power,
        out_shape=(
            VMEM((4, 4 * TAPS, 2 * templates), BF16),
            VMEM((8, LANES), F32),
            VMEM((slots, HALF, LANES), F32),
            VMEM((tiles, HALF, LANES), F32),
        ),
        in_specs=[pl.BlockSpec(memory_space=pltpu.SMEM), pl.BlockSpec(memory_space=VMEM)],
        scratch_shapes=[
            VMEM((2, 3, 16, LANES), F32),
            VMEM((4, 2 * LANES, 2 * LANES), BF16),
            VMEM((slots, HALF + 8, LANES), F32),
            VMEM((slots, HALF + 8, LANES), F32),
        ],
        compiler_params=pltpu.CompilerParams(vmem_limit_bytes=32 << 20),
        name="inner_power",
    )(pltpu.with_memory_space_constraint(wing_width, pltpu.HBM), near(packed))
    sent = pl.pallas_call(
        functools.partial(segment_sums, 1.0 / (4 * segments)),
        out_shape=VMEM((peers, fine, here), BF16),
        scratch_shapes=[
            VMEM((2, 2, 16, LANES), F32),
            VMEM((4, LANES, 2 * LANES), BF16),
            VMEM((slots, HALF + 8, LANES), F32),
            VMEM((slots, HALF + 8, LANES), F32),
            VMEM((tiles, HALF, LANES), F32),
        ] + [VMEM((LANES, LANES), F32)] * slots,
        compiler_params=pltpu.CompilerParams(vmem_limit_bytes=32 << 20),
        name="segment_sums",
    )(*[near(z) for z in (packed, halo, reach, taps, middle, inner)])
    recv = lax.all_to_all(sent, "seg", 0, 0, tiled=True)
    halves = jnp.sum(recv.astype(F32).reshape(peers // 2, 2, fine, here), 0)
    return jnp.concatenate([halves[0], halves[1]], 1)


def solution(mesh):
    placed = (
        P("seg", None, None, "band"),
        P("seg", None),
        P("seg", None, None, None),
        P("seg", None),
        P("seg", None),
        P(),
    )
    return jax.shard_map(
        per_device, mesh=mesh, in_specs=placed, out_specs=P("seg", "band"), check_vma=False
    )
```

time: 30 us -> 29.4 us (0.980)
  blocking collectives: 21.5 us -> 20.7 us
    pallas_call x1, Pallas kernels: 1.76 us -> 2.56 us  [per_device(): pl.pallas_call(inner_power, out_shape=(VMEM((4, 4 * TAPS, 2 * templates),...]
    all_to_all x1, blocking collectives: 19.3 us -> 18.5 us  [per_device(): recv = lax.all_to_all(sent, 'seg', 0, 0, tiled=True)]
    pallas_call x1, Pallas kernels: 1.71 us -> 1.11 us  [per_device(): pl.pallas_call(functools.partial(segment_sums, 1.0 / (4 * segments)), out...]
  transfers between devices with their start and end apart: 1 -> 1, of which waited for: 0 -> 0; matrix products, arithmetic and copies ran while one was open for 0% -> 0% of each run, Pallas kernels for 6% -> 9%
where the time goes in v5:
time: 29.4 us; the launch traced here: 29.2 us
  blocking collectives  20.7 us (70%)
  Pallas kernels  4.45 us (15%)
  starting transfers between devices  3.35 us (11%)
  other arithmetic  0.64 us (2%)
    all_to_all x1, blocking collectives, per_device(): recv = lax.all_to_all(sent, 'seg', 0, 0, tiled=True)  18.5 us
    ppermute x1, starting transfers between devices, per_device(): halo = lax.ppermute(rows, ('seg', 'band'), swap)  3.35 us
    pallas_call x1, Pallas kernels, per_device(): pl.pallas_call(inner_power, out_shape=(VMEM((4, 4 * TAPS, 2 * templates),...  2.56 us
    all_gather x1, blocking collectives, per_device(): lax.all_gather(packed[None], 'seg', axis=0, tiled=True, axis_index_groups...  2.2 us
    pallas_call x1, Pallas kernels, per_device(): pl.pallas_call(functools.partial(segment_sums, 1.0 / (4 * segments)), out...  1.11 us
    pallas_call x1, Pallas kernels, per_device(): pl.pallas_call(pack, out_shape=VMEM((PACKED_ROWS, templates), F32), name=...  0.78 us
    concatenate x1, other arithmetic, per_device(): return jnp.concatenate([halves[0], halves[1]], 1)  0.62 us
  transfers between devices with their start and end apart: 1, of which 0 were waited for; matrix products, arithmetic and copies ran while one was open for 0% of the time, Pallas kernels for 9%

profile of v5, /device:TPU:257, one launch (start us, length us, event | category | flops | bytes accessed | tf_op | source)
XLA Modules:
  0.0 29.2 jit_solution(16796829725368844121)
XLA Ops:
  0.0 0.8 %pack.1 = f32[24,512]{1,0:T(8,128)S(1)} custom-call(bf16[2,2,2,256]{3,2,1,0:T(2,128)(2,1)} %sft_ref.1, f32[2,512]{1,0:T(2,128)} %doppler_ref.1, f32[2,2,2,512]{3,2,1,0:T(2,128)} %antenna_ref.1, s32[2,512]{1,0:T(2,128)} %index_ref.1, s32[2,512]{1,0:T(2,128)} %offset_ref.1), custom_call_target="tpu_custom_call" | custom-call | tf_op jit(solution)/shard_map/pack/pallas_call | solution.py:299
  0.8 2.2 %all-gather = f32[48,512]{1,0:T(8,128)S(1)} all-gather(f32[24,512]{1,0:T(8,128)S(1)} %pack.1), channel_id=2, replica_groups={{0,32},{64,96},{128,160},{192,224},{256,288},{320,352},{384,416},{448,4..., dimensions={0}, use_global_device_ids=true | all-gather | bytes 147456 | tf_op jit(solution)/shard_map/all_gather | solution.py:303
  3.0 3.3 %collective-permute-start = (bf16[2,8,256]{2,1,0:T(8,128)(2,1)S(1)}, bf16[2,8,256]{2,1,0:T(8,128)(2,1)S(1)}, u32[]{:S(2)}, u32[]{:S(2)}) collective-permute-start(bf16[2,8,256]{2,1,0:T(8,128)(2,1)S(1)} %slice.19), channel_id=1, source_target_pairs={{1,32},{32,1},{2,33},{33,2},{3,34},{34,3},{4,35},{35,4},{5,36},{36... | collective-permute-start | bytes 24584 | tf_op jit(solution)/shard_map/ppermute | solution.py:309
  6.3 2.6 %inner_power.1 = (bf16[4,256,1024]{2,1,0:T(8,128)(2,1)S(1)}, f32[8,128]{1,0:T(8,128)S(1)}, f32[16,64,128]{2,1,0:T(8,128)S(1)}, f32[4,64,128]{2,1,0:T(8,128)S(1)}) custom-call(s32[32]{0:T(128)} %wing_ref.1, f32[2,24,512]{2,1,0:T(8,128)S(1)} %bitcast.8), custom_call_target="tpu_custom_call" | custom-call | tf_op jit(solution)/shard_map/inner_power/pallas_call | solution.py:311
  8.9 0.0 collective-permute-done.halo_ref
  8.9 1.1 %segment_sums.1 = bf16[16,32,128]{2,1,0:T(8,128)(2,1)S(1)} custom-call(f32[2,24,512]{2,1,0:T(8,128)S(1)} %bitcast.9, bf16[2,8,256]{2,1,0:T(8,128)(2,1)S(1)} %collective-permute-done.halo_ref, f32[8,128]{1,0:T(8,128)S(1)} %get-tuple-element.9.reach_ref, bf16[4,256,1024]{2,1,0:T(8,128)(2,1)S(1)} %get-tuple-element.10.taps_ref, ...), custom_call_target="tpu_custom_call" | custom-call | tf_op jit(solution)/shard_map/segment_sums/pallas_call | solution.py:329
  10.0 18.5 %all_to_all.5 = bf16[16,32,128]{2,1,0:T(8,128)(2,1)S(1)} all-to-all(bf16[16,32,128]{2,1,0:T(8,128)(2,1)S(1)} %segment_sums.1), channel_id=1, replica_groups=mesh['seg'=16,'band'=32] {'seg'}, dimensions={0} | all-to-all | bytes 262144 | tf_op jit(solution)/shard_map/all_to_all | solution.py:342
  28.6 0.6 %pad_maximum_fusion = f32[32,256]{1,0:T(8,128)} fusion(f32[32,128]{1,0:T(8,128)S(1)} %get-tuple-element.14, f32[32,128]{1,0:T(8,128)S(1)} %get-tuple-element.13), kind=kLoop, calls=%fused_computation.1 | loop fusion | flops 8192 | bytes 65536 | tf_op jit(solution)/shard_map/concatenate | solution.py:344
  (3 shorter events, 0.0 us)
Async XLA Ops:
  3.0 5.9 %collective-permute-start = (bf16[2,8,256]{2,1,0:T(8,128)(2,1)S(1)}, bf16[2,8,256]{2,1,0:T(8,128)(2,1)S(1)}, u32[]{:S(2)}, u32[]{:S(2)}) collective-permute-start(bf16[2,8,256]{2,1,0:T(8,128)(2,1)S(1)} %slice.19), channel_id=1, source_target_pairs={{1,32},{32,1},{2,33},{33,2},{3,34},{34,3},{4,35},{35,4},{5,36},{36... | collective-permute-start | bytes 24584 | tf_op jit(solution)/shard_map/ppermute | solution.py:309

commit v6 on v5

--- a/solution.py
+++ b/solution.py
@@ -53,7 +53,18 @@
     return sine * r, cosine
 
 
-def pack(sft_ref, doppler_ref, antenna_ref, index_ref, offset_ref, out_ref):
+def pack(wing_ref, sft_ref, doppler_ref, antenna_ref, index_ref, offset_ref, out_ref, reach_ref):
+    band = lax.axis_index("band")
+    last = lax.axis_size("band") - 1
+    core = lax.rem(lax.axis_index("seg"), 2)
+    beside = jnp.where(core == 0, band - 1, band + 1)
+    w_own = wing_ref[band]
+    w_beside = wing_ref[jnp.clip(beside, 0, last)]
+    w_beside = jnp.where((beside < 0) | (beside > last), 0, w_beside)
+    row = row_iota(reach_ref.shape)
+    reach = jnp.where((row == 0) & (core == 0) | (row == 2) & (core == 1), w_beside, w_own)
+    reach_ref[...] = reach.astype(F32)
+
     bins = sft_ref.shape[3]
     out_ref[...] = jnp.zeros_like(out_ref)
     for s in range(2):
@@ -160,21 +171,10 @@
 
 
 def inner_power(
-    wing_ref, packed_ref, taps_ref, reach_ref, middle_ref, total_ref,
+    packed_ref, reach_ref, taps_ref, middle_ref, total_ref,
     chunk_ref, t_ref, u_ref, v_ref
 ):
-    band = lax.axis_index("band")
-    last = lax.axis_size("band") - 1
-    core = lax.rem(lax.axis_index("seg"), 2)
-    first = core == 0
-    beside = jnp.where(first, band - 1, band + 1)
-    w_own = wing_ref[band]
-    w_beside = wing_ref[jnp.clip(beside, 0, last)]
-    w_beside = jnp.where((beside < 0) | (beside > last), 0, w_beside)
-    row = row_iota(reach_ref.shape)
-    reach = jnp.where((row == 0) & (core == 0) | (row == 2) & (core == 1), w_beside, w_own)
-    reach_ref[...] = reach.astype(F32)
-
+    first = lax.rem(lax.axis_index("seg"), 2) == 0
     templates = packed_ref.shape[2]
     tap = (WMAX - 1) - row_iota((TAPS, LANES)).astype(F32)
     for seg in range(4):
@@ -220,7 +220,7 @@
     for i, (even, odd) in enumerate(halves):
         for place in range(2):
             chunk_ref[place, i] = jnp.where(first, even[place], odd[place])
-    near_reach = [tap_center() < w_own.astype(F32)] * 8
+    near_reach = [tap_center() < reach_ref[1:2, :]] * 8
     tiles = templates // LANES
     for seg in range(4):
         for ri in range(2):
@@ -239,7 +239,7 @@
 
 def segment_sums(
     scale, packed_ref, halo_ref, reach_ref, taps_ref, middle_ref, total_ref, out_ref,
-    chunk_ref, t_ref, u_ref, v_ref, acc_ref, *p_refs
+    chunk_ref, t_ref, u_ref, v_ref, acc_ref
 ):
     bins = out_ref.shape[2]
     segs = taps_ref.shape[0]
@@ -260,8 +260,6 @@
         chunk_ref[1, i] = high
     center = tap_center()
     below, above = (center < reach_ref[i : i + 1, :] for i in (0, 2))
-    edge_start = pl.multiple_of(jnp.where(first, 0, HALF), 8)
-    middle_start = pl.multiple_of(jnp.where(first, HALF, 0), 8)
 
     tiles = taps_ref.shape[2] // (2 * LANES)
     each = LANES // out_ref.shape[1]
@@ -271,11 +269,12 @@
     for seg in range(segs):
         for tile in range(tiles):
             slot = seg * tiles + tile
-            p_refs[slot][pl.ds(middle_start, HALF), :] = middle_ref[slot]
-            p_refs[slot][pl.ds(edge_start, HALF), :] = power_of(
+            power = power_of(
                 t_ref[seg], taps_ref[seg, :, tile * 2 * LANES : (tile + 1) * 2 * LANES]
             )
-            parts = [p_refs[slot][8 * t : 8 * t + 8, :] for t in range(LANES // 8)]
+            middle = middle_ref[slot]
+            parts = [jnp.where(first, power, middle), jnp.where(first, middle, power)]
+            parts = [part[8 * t : 8 * t + 8] for part in parts for t in range(HALF // 8)]
             values = shifted(parts, packed_ref, seg, tile, u_ref.at[slot], v_ref.at[slot])
             add_tiles(acc_ref, tile, values, seg == 0)
             if seg == segs - 1:
@@ -296,9 +295,12 @@
     segments = sft.shape[0] * peers
     tiles = templates // LANES
     here = bins // 2
-    packed = pl.pallas_call(
-        pack, out_shape=VMEM((PACKED_ROWS, templates), F32), name="pack"
-    )(sft, doppler, antenna, coarse_index, freq_offset)
+    packed, reach = pl.pallas_call(
+        pack,
+        out_shape=(VMEM((PACKED_ROWS, templates), F32), VMEM((8, LANES), F32)),
+        in_specs=[pl.BlockSpec(memory_space=pltpu.SMEM)] + [pl.BlockSpec(memory_space=VMEM)] * 5,
+        name="pack",
+    )(wing_width, sft, doppler, antenna, coarse_index, freq_offset)
     pairs = [[i, i + 1] for i in range(0, peers, 2)]
     packed = lax.all_gather(packed[None], "seg", axis=0, tiled=True, axis_index_groups=pairs)
     rows = packed[:, BIN_ROW:, :bins].astype(BF16)
@@ -308,15 +310,13 @@
             swap += [(low * count + b, high * count + b - 1), (high * count + b - 1, low * count + b)]
     halo = lax.ppermute(rows, ("seg", "band"), swap)
     slots = 4 * tiles
-    taps, reach, middle, inner = pl.pallas_call(
+    taps, middle, inner = pl.pallas_call(
         inner_power,
         out_shape=(
             VMEM((4, 4 * TAPS, 2 * templates), BF16),
-            VMEM((8, LANES), F32),
             VMEM((slots, HALF, LANES), F32),
             VMEM((tiles, HALF, LANES), F32),
         ),
-        in_specs=[pl.BlockSpec(memory_space=pltpu.SMEM), pl.BlockSpec(memory_space=VMEM)],
         scratch_shapes=[
             VMEM((2, 3, 16, LANES), F32),
             VMEM((4, 2 * LANES, 2 * LANES), BF16),
@@ -325,7 +325,7 @@
         ],
         compiler_params=pltpu.CompilerParams(vmem_limit_bytes=32 << 20),
         name="inner_power",
-    )(pltpu.with_memory_space_constraint(wing_width, pltpu.HBM), near(packed))
+    )(near(packed), near(reach))
     sent = pl.pallas_call(
         functools.partial(segment_sums, 1.0 / (4 * segments)),
         out_shape=VMEM((peers, fine, here), BF16),
@@ -335,7 +335,7 @@
             VMEM((slots, HALF + 8, LANES), F32),
             VMEM((slots, HALF + 8, LANES), F32),
             VMEM((tiles, HALF, LANES), F32),
-        ] + [VMEM((LANES, LANES), F32)] * slots,
+        ],
         compiler_params=pltpu.CompilerParams(vmem_limit_bytes=32 << 20),
         name="segment_sums",
     )(*[near(z) for z in (packed, halo, reach, taps, middle, inner)])

time: 29.4 us -> 29.4 us (level)
  blocking collectives: 20.7 us -> 21.4 us
  Pallas kernels: 4.45 us -> 3.82 us
    pallas_call x1, Pallas kernels: 2.56 us -> 1.9 us  [per_device(): pl.pallas_call(inner_power, out_shape=(VMEM((4, 4 * TAPS, 2 * templates),...]
    all_to_all x1, blocking collectives: 18.5 us -> 19.2 us  [per_device(): recv = lax.all_to_all(sent, 'seg', 0, 0, tiled=True)]
  transfers between devices with their start and end apart: 1 -> 1, of which waited for: 0 -> 0; matrix products, arithmetic and copies ran while one was open for 0% -> 0% of each run, Pallas kernels for 9% -> 7%
where the time goes in v6:
time: 29.4 us; the launch traced here: 29.2 us
  blocking collectives  21.4 us (73%)
  Pallas kernels  3.82 us (13%)
  starting transfers between devices  3.35 us (11%)
  other arithmetic  0.64 us (2%)
    all_to_all x1, blocking collectives, per_device(): recv = lax.all_to_all(sent, 'seg', 0, 0, tiled=True)  19.2 us
    ppermute x1, starting transfers between devices, per_device(): halo = lax.ppermute(rows, ('seg', 'band'), swap)  3.35 us
    all_gather x1, blocking collectives, per_device(): lax.all_gather(packed[None], 'seg', axis=0, tiled=True, axis_index_groups...  2.2 us
    pallas_call x1, Pallas kernels, per_device(): pl.pallas_call(inner_power, out_shape=(VMEM((4, 4 * TAPS, 2 * templates),...  1.9 us
    pallas_call x1, Pallas kernels, per_device(): pl.pallas_call(functools.partial(segment_sums, 1.0 / (4 * segments)), out...  1.09 us
    pallas_call x1, Pallas kernels, per_device(): pl.pallas_call(pack, out_shape=(VMEM((PACKED_ROWS, templates), F32), VMEM...  0.83 us
    concatenate x1, other arithmetic, per_device(): return jnp.concatenate([halves[0], halves[1]], 1)  0.62 us
  transfers between devices with their start and end apart: 1, of which 0 were waited for; matrix products, arithmetic and copies ran while one was open for 0% of the time, Pallas kernels for 7%

profile of v6, /device:TPU:257, one launch (start us, length us, event | category | flops | bytes accessed | tf_op | source)
XLA Modules:
  0.0 29.2 jit_solution(3510726764283460471)
XLA Ops:
  0.0 0.8 %pack.1 = (f32[24,512]{1,0:T(8,128)S(1)}, f32[8,128]{1,0:T(8,128)S(1)}) custom-call(s32[32]{0:T(128)} %wing_ref.1, bf16[2,2,2,256]{3,2,1,0:T(2,128)(2,1)} %sft_ref.1, f32[2,512]{1,0:T(2,128)} %doppler_ref.1, f32[2,2,2,512]{3,2,1,0:T(2,128)} %antenna_ref.1, s32[2,512]{1,0:T(2,128)} %index_ref.1, s32[2,512]{1,0:T(2,128)} %offset_ref.1), custom_call_target="tpu_custom_call" | custom-call | tf_op jit(solution)/shard_map/pack/pallas_call | solution.py:298
  0.8 2.2 %all-gather = f32[48,512]{1,0:T(8,128)S(1)} all-gather(f32[24,512]{1,0:T(8,128)S(1)} %get-tuple-element.10), channel_id=2, replica_groups={{0,32},{64,96},{128,160},{192,224},{256,288},{320,352},{384,416},{448,4..., dimensions={0}, use_global_device_ids=true | all-gather | bytes 147456 | tf_op jit(solution)/shard_map/all_gather | solution.py:305
  3.0 3.3 %collective-permute-start = (bf16[2,8,256]{2,1,0:T(8,128)(2,1)S(1)}, bf16[2,8,256]{2,1,0:T(8,128)(2,1)S(1)}, u32[]{:S(2)}, u32[]{:S(2)}) collective-permute-start(bf16[2,8,256]{2,1,0:T(8,128)(2,1)S(1)} %slice.19), channel_id=1, source_target_pairs={{1,32},{32,1},{2,33},{33,2},{3,34},{34,3},{4,35},{35,4},{5,36},{36... | collective-permute-start | bytes 24584 | tf_op jit(solution)/shard_map/ppermute | solution.py:311
  6.4 1.9 %inner_power.1 = (bf16[4,256,1024]{2,1,0:T(8,128)(2,1)S(1)}, f32[16,64,128]{2,1,0:T(8,128)S(1)}, f32[4,64,128]{2,1,0:T(8,128)S(1)}) custom-call(f32[2,24,512]{2,1,0:T(8,128)S(1)} %bitcast.8, f32[8,128]{1,0:T(8,128)S(1)} %get-tuple-element.11.reach_ref), custom_call_target="tpu_custom_call" | custom-call | tf_op jit(solution)/shard_map/inner_power/pallas_call | solution.py:313
  8.3 0.0 collective-permute-done.halo_ref
  8.3 1.1 %segment_sums.1 = bf16[16,32,128]{2,1,0:T(8,128)(2,1)S(1)} custom-call(f32[2,24,512]{2,1,0:T(8,128)S(1)} %bitcast.9, bf16[2,8,256]{2,1,0:T(8,128)(2,1)S(1)} %collective-permute-done.halo_ref, f32[8,128]{1,0:T(8,128)S(1)} %get-tuple-element.11.reach_ref, bf16[4,256,1024]{2,1,0:T(8,128)(2,1)S(1)} %get-tuple-element.12.taps_ref, ...), custom_call_target="tpu_custom_call" | custom-call | tf_op jit(solution)/shard_map/segment_sums/pallas_call | solution.py:329
  9.4 19.2 %all_to_all.5 = bf16[16,32,128]{2,1,0:T(8,128)(2,1)S(1)} all-to-all(bf16[16,32,128]{2,1,0:T(8,128)(2,1)S(1)} %segment_sums.1), channel_id=1, replica_groups=mesh['seg'=16,'band'=32] {'seg'}, dimensions={0} | all-to-all | bytes 262144 | tf_op jit(solution)/shard_map/all_to_all | solution.py:342
  28.6 0.6 %pad_maximum_fusion = f32[32,256]{1,0:T(8,128)} fusion(f32[32,128]{1,0:T(8,128)S(1)} %get-tuple-element.16, f32[32,128]{1,0:T(8,128)S(1)} %get-tuple-element.15), kind=kLoop, calls=%fused_computation.1 | loop fusion | flops 8192 | bytes 65536 | tf_op jit(solution)/shard_map/concatenate | solution.py:344
  (3 shorter events, 0.0 us)
Async XLA Ops:
  3.0 5.3 %collective-permute-start = (bf16[2,8,256]{2,1,0:T(8,128)(2,1)S(1)}, bf16[2,8,256]{2,1,0:T(8,128)(2,1)S(1)}, u32[]{:S(2)}, u32[]{:S(2)}) collective-permute-start(bf16[2,8,256]{2,1,0:T(8,128)(2,1)S(1)} %slice.19), channel_id=1, source_target_pairs={{1,32},{32,1},{2,33},{33,2},{3,34},{34,3},{4,35},{35,4},{5,36},{36... | collective-permute-start | bytes 24584 | tf_op jit(solution)/shard_map/ppermute | solution.py:311

commit v7 on v5

--- a/solution.py
+++ b/solution.py
@@ -239,7 +239,7 @@
 
 def segment_sums(
     scale, packed_ref, halo_ref, reach_ref, taps_ref, middle_ref, total_ref, out_ref,
-    chunk_ref, t_ref, u_ref, v_ref, acc_ref, *p_refs
+    chunk_ref, t_ref, u_ref, v_ref, acc_ref
 ):
     bins = out_ref.shape[2]
     segs = taps_ref.shape[0]
@@ -260,8 +260,6 @@
         chunk_ref[1, i] = high
     center = tap_center()
     below, above = (center < reach_ref[i : i + 1, :] for i in (0, 2))
-    edge_start = pl.multiple_of(jnp.where(first, 0, HALF), 8)
-    middle_start = pl.multiple_of(jnp.where(first, HALF, 0), 8)
 
     tiles = taps_ref.shape[2] // (2 * LANES)
     each = LANES // out_ref.shape[1]
@@ -271,11 +269,12 @@
     for seg in range(segs):
         for tile in range(tiles):
             slot = seg * tiles + tile
-            p_refs[slot][pl.ds(middle_start, HALF), :] = middle_ref[slot]
-            p_refs[slot][pl.ds(edge_start, HALF), :] = power_of(
+            power = power_of(
                 t_ref[seg], taps_ref[seg, :, tile * 2 * LANES : (tile + 1) * 2 * LANES]
             )
-            parts = [p_refs[slot][8 * t : 8 * t + 8, :] for t in range(LANES // 8)]
+            middle = middle_ref[slot]
+            parts = [jnp.where(first, power, middle), jnp.where(first, middle, power)]
+            parts = [part[8 * t : 8 * t + 8] for part in parts for t in range(HALF // 8)]
             values = shifted(parts, packed_ref, seg, tile, u_ref.at[slot], v_ref.at[slot])
             add_tiles(acc_ref, tile, values, seg == 0)
             if seg == segs - 1:
@@ -335,7 +334,7 @@
             VMEM((slots, HALF + 8, LANES), F32),
             VMEM((slots, HALF + 8, LANES), F32),
             VMEM((tiles, HALF, LANES), F32),
-        ] + [VMEM((LANES, LANES), F32)] * slots,
+        ],
         compiler_params=pltpu.CompilerParams(vmem_limit_bytes=32 << 20),
         name="segment_sums",
     )(*[near(z) for z in (packed, halo, reach, taps, middle, inner)])

time: 29.4 us -> 29.4 us (level)
  no operation moved by 1% of the time
where the time goes in v7:
time: 29.4 us; the launch traced here: 29.2 us
  blocking collectives  20.7 us (70%)
  Pallas kernels  4.42 us (15%)
  starting transfers between devices  3.35 us (11%)
  other arithmetic  0.64 us (2%)
    all_to_all x1, blocking collectives, per_device(): recv = lax.all_to_all(sent, 'seg', 0, 0, tiled=True)  18.5 us
    ppermute x1, starting transfers between devices, per_device(): halo = lax.ppermute(rows, ('seg', 'band'), swap)  3.35 us
    pallas_call x1, Pallas kernels, per_device(): pl.pallas_call(inner_power, out_shape=(VMEM((4, 4 * TAPS, 2 * templates),...  2.56 us
    all_gather x1, blocking collectives, per_device(): lax.all_gather(packed[None], 'seg', axis=0, tiled=True, axis_index_groups...  2.2 us
    pallas_call x1, Pallas kernels, per_device(): pl.pallas_call(functools.partial(segment_sums, 1.0 / (4 * segments)), out...  1.08 us
    pallas_call x1, Pallas kernels, per_device(): pl.pallas_call(pack, out_shape=VMEM((PACKED_ROWS, templates), F32), name=...  0.78 us
    concatenate x1, other arithmetic, per_device(): return jnp.concatenate([halves[0], halves[1]], 1)  0.62 us
  transfers between devices with their start and end apart: 1, of which 0 were waited for; matrix products, arithmetic and copies ran while one was open for 0% of the time, Pallas kernels for 9%

profile of v7, /device:TPU:257, one launch (start us, length us, event | category | flops | bytes accessed | tf_op | source)
XLA Modules:
  0.0 29.2 jit_solution(13072187184564618166)
XLA Ops:
  0.0 0.8 %pack.1 = f32[24,512]{1,0:T(8,128)S(1)} custom-call(bf16[2,2,2,256]{3,2,1,0:T(2,128)(2,1)} %sft_ref.1, f32[2,512]{1,0:T(2,128)} %doppler_ref.1, f32[2,2,2,512]{3,2,1,0:T(2,128)} %antenna_ref.1, s32[2,512]{1,0:T(2,128)} %index_ref.1, s32[2,512]{1,0:T(2,128)} %offset_ref.1), custom_call_target="tpu_custom_call" | custom-call | tf_op jit(solution)/shard_map/pack/pallas_call | solution.py:298
  0.8 2.2 %all-gather = f32[48,512]{1,0:T(8,128)S(1)} all-gather(f32[24,512]{1,0:T(8,128)S(1)} %pack.1), channel_id=2, replica_groups={{0,32},{64,96},{128,160},{192,224},{256,288},{320,352},{384,416},{448,4..., dimensions={0}, use_global_device_ids=true | all-gather | bytes 147456 | tf_op jit(solution)/shard_map/all_gather | solution.py:302
  3.0 3.3 %collective-permute-start = (bf16[2,8,256]{2,1,0:T(8,128)(2,1)S(1)}, bf16[2,8,256]{2,1,0:T(8,128)(2,1)S(1)}, u32[]{:S(2)}, u32[]{:S(2)}) collective-permute-start(bf16[2,8,256]{2,1,0:T(8,128)(2,1)S(1)} %slice.19), channel_id=1, source_target_pairs={{1,32},{32,1},{2,33},{33,2},{3,34},{34,3},{4,35},{35,4},{5,36},{36... | collective-permute-start | bytes 24584 | tf_op jit(solution)/shard_map/ppermute | solution.py:308
  6.3 2.6 %inner_power.1 = (bf16[4,256,1024]{2,1,0:T(8,128)(2,1)S(1)}, f32[8,128]{1,0:T(8,128)S(1)}, f32[16,64,128]{2,1,0:T(8,128)S(1)}, f32[4,64,128]{2,1,0:T(8,128)S(1)}) custom-call(s32[32]{0:T(128)} %wing_ref.1, f32[2,24,512]{2,1,0:T(8,128)S(1)} %bitcast.8), custom_call_target="tpu_custom_call" | custom-call | tf_op jit(solution)/shard_map/inner_power/pallas_call | solution.py:310
  8.9 0.0 collective-permute-done.halo_ref
  8.9 1.1 %segment_sums.1 = bf16[16,32,128]{2,1,0:T(8,128)(2,1)S(1)} custom-call(f32[2,24,512]{2,1,0:T(8,128)S(1)} %bitcast.9, bf16[2,8,256]{2,1,0:T(8,128)(2,1)S(1)} %collective-permute-done.halo_ref, f32[8,128]{1,0:T(8,128)S(1)} %get-tuple-element.9.reach_ref, bf16[4,256,1024]{2,1,0:T(8,128)(2,1)S(1)} %get-tuple-element.10.taps_ref, ...), custom_call_target="tpu_custom_call" | custom-call | tf_op jit(solution)/shard_map/segment_sums/pallas_call | solution.py:328
  10.0 18.5 %all_to_all.5 = bf16[16,32,128]{2,1,0:T(8,128)(2,1)S(1)} all-to-all(bf16[16,32,128]{2,1,0:T(8,128)(2,1)S(1)} %segment_sums.1), channel_id=1, replica_groups=mesh['seg'=16,'band'=32] {'seg'}, dimensions={0} | all-to-all | bytes 262144 | tf_op jit(solution)/shard_map/all_to_all | solution.py:341
  28.5 0.6 %pad_maximum_fusion = f32[32,256]{1,0:T(8,128)} fusion(f32[32,128]{1,0:T(8,128)S(1)} %get-tuple-element.14, f32[32,128]{1,0:T(8,128)S(1)} %get-tuple-element.13), kind=kLoop, calls=%fused_computation.1 | loop fusion | flops 8192 | bytes 65536 | tf_op jit(solution)/shard_map/concatenate | solution.py:343
  (3 shorter events, 0.0 us)
Async XLA Ops:
  3.0 5.9 %collective-permute-start = (bf16[2,8,256]{2,1,0:T(8,128)(2,1)S(1)}, bf16[2,8,256]{2,1,0:T(8,128)(2,1)S(1)}, u32[]{:S(2)}, u32[]{:S(2)}) collective-permute-start(bf16[2,8,256]{2,1,0:T(8,128)(2,1)S(1)} %slice.19), channel_id=1, source_target_pairs={{1,32},{32,1},{2,33},{33,2},{3,34},{34,3},{4,35},{35,4},{5,36},{36... | collective-permute-start | bytes 24584 | tf_op jit(solution)/shard_map/ppermute | solution.py:308

commit v8 on v5

--- a/solution.py
+++ b/solution.py
@@ -244,15 +244,10 @@
     bins = out_ref.shape[2]
     segs = taps_ref.shape[0]
     first = lax.rem(lax.axis_index("seg"), 2) == 0
-    halo = [
-        jnp.concatenate(
-            [halo_ref[side, :, c * LANES : (c + 1) * LANES].astype(F32) for side in range(2)], 0
-        )
-        for c in range(2)
-    ]
+    halo = jnp.concatenate([halo_ref[side].astype(F32) for side in range(2)], 0)
     parts = [
-        jnp.where(first, own_bins(packed_ref, 0), halo[0]),
-        jnp.where(first, halo[1], own_bins(packed_ref, 1)),
+        jnp.where(first, own_bins(packed_ref, 0), halo),
+        jnp.where(first, halo, own_bins(packed_ref, 1)),
     ]
     flipped, swapped = mirrored(parts)
     for i, (low, high) in enumerate(((swapped[0], flipped[0]), (flipped[1], swapped[1]))):
@@ -301,7 +296,9 @@
     )(sft, doppler, antenna, coarse_index, freq_offset)
     pairs = [[i, i + 1] for i in range(0, peers, 2)]
     packed = lax.all_gather(packed[None], "seg", axis=0, tiled=True, axis_index_groups=pairs)
-    rows = packed[:, BIN_ROW:, :bins].astype(BF16)
+    even = lax.axis_index("seg") % 2 == 0
+    rows = jnp.where(even, packed[:, BIN_ROW:, :LANES], packed[:, BIN_ROW:, bins - LANES : bins])
+    rows = rows.astype(BF16)
     swap = []
     for low, high in pairs:
         for b in range(1, count):

time: 29.4 us -> 29.4 us (level)
  no operation moved by 1% of the time
where the time goes in v8:
time: 29.4 us; the launch traced here: 29.2 us
  blocking collectives  20.7 us (70%)
  Pallas kernels  4.44 us (15%)
  starting transfers between devices  3.35 us (11%)
  other arithmetic  0.65 us (2%)
    all_to_all x1, blocking collectives, per_device(): recv = lax.all_to_all(sent, 'seg', 0, 0, tiled=True)  18.5 us
    ppermute x1, starting transfers between devices, per_device(): halo = lax.ppermute(rows, ('seg', 'band'), swap)  3.35 us
    pallas_call x1, Pallas kernels, per_device(): pl.pallas_call(inner_power, out_shape=(VMEM((4, 4 * TAPS, 2 * templates),...  2.55 us
    all_gather x1, blocking collectives, per_device(): lax.all_gather(packed[None], 'seg', axis=0, tiled=True, axis_index_groups...  2.2 us
    pallas_call x1, Pallas kernels, per_device(): pl.pallas_call(functools.partial(segment_sums, 1.0 / (4 * segments)), out...  1.11 us
    pallas_call x1, Pallas kernels, per_device(): pl.pallas_call(pack, out_shape=VMEM((PACKED_ROWS, templates), F32), name=...  0.78 us
    concatenate x1, other arithmetic, per_device(): return jnp.concatenate([halves[0], halves[1]], 1)  0.62 us
  transfers between devices with their start and end apart: 1, of which 0 were waited for; matrix products, arithmetic and copies ran while one was open for 0% of the time, Pallas kernels for 9%

profile of v8, /device:TPU:257, one launch (start us, length us, event | category | flops | bytes accessed | tf_op | source)
XLA Modules:
  0.0 29.2 jit_solution(10391634600385524126)
XLA Ops:
  0.0 0.8 %pack.1 = f32[24,512]{1,0:T(8,128)S(1)} custom-call(bf16[2,2,2,256]{3,2,1,0:T(2,128)(2,1)} %sft_ref.1, f32[2,512]{1,0:T(2,128)} %doppler_ref.1, f32[2,2,2,512]{3,2,1,0:T(2,128)} %antenna_ref.1, s32[2,512]{1,0:T(2,128)} %index_ref.1, s32[2,512]{1,0:T(2,128)} %offset_ref.1), custom_call_target="tpu_custom_call" | custom-call | tf_op jit(solution)/shard_map/pack/pallas_call | solution.py:294
  0.8 2.2 %all-gather = f32[48,512]{1,0:T(8,128)S(1)} all-gather(f32[24,512]{1,0:T(8,128)S(1)} %pack.1), channel_id=2, replica_groups={{0,32},{64,96},{128,160},{192,224},{256,288},{320,352},{384,416},{448,4..., dimensions={0}, use_global_device_ids=true | all-gather | bytes 147456 | tf_op jit(solution)/shard_map/all_gather | solution.py:298
  3.0 3.3 %collective-permute-start = (bf16[2,8,128]{2,1,0:T(8,128)(2,1)S(1)}, bf16[2,8,128]{2,1,0:T(8,128)(2,1)S(1)}, u32[]{:S(2)}, u32[]{:S(2)}) collective-permute-start(bf16[2,8,128]{2,1,0:T(8,128)(2,1)S(1)} %fusion), channel_id=1, source_target_pairs={{1,32},{32,1},{2,33},{33,2},{3,34},{34,3},{4,35},{35,4},{5,36},{36... | collective-permute-start | bytes 12296 | tf_op jit(solution)/shard_map/ppermute | solution.py:306
  6.3 2.5 %inner_power.1 = (bf16[4,256,1024]{2,1,0:T(8,128)(2,1)S(1)}, f32[8,128]{1,0:T(8,128)S(1)}, f32[16,64,128]{2,1,0:T(8,128)S(1)}, f32[4,64,128]{2,1,0:T(8,128)S(1)}) custom-call(s32[32]{0:T(128)} %wing_ref.1, f32[2,24,512]{2,1,0:T(8,128)S(1)} %bitcast.8), custom_call_target="tpu_custom_call" | custom-call | tf_op jit(solution)/shard_map/inner_power/pallas_call | solution.py:308
  8.9 0.0 collective-permute-done.halo_ref
  8.9 1.1 %segment_sums.1 = bf16[16,32,128]{2,1,0:T(8,128)(2,1)S(1)} custom-call(f32[2,24,512]{2,1,0:T(8,128)S(1)} %bitcast.9, bf16[2,8,128]{2,1,0:T(8,128)(2,1)S(1)} %collective-permute-done.halo_ref, f32[8,128]{1,0:T(8,128)S(1)} %get-tuple-element.9.reach_ref, bf16[4,256,1024]{2,1,0:T(8,128)(2,1)S(1)} %get-tuple-element.10.taps_ref, ...), custom_call_target="tpu_custom_call" | custom-call | tf_op jit(solution)/shard_map/segment_sums/pallas_call | solution.py:326
  10.0 18.5 %all_to_all.5 = bf16[16,32,128]{2,1,0:T(8,128)(2,1)S(1)} all-to-all(bf16[16,32,128]{2,1,0:T(8,128)(2,1)S(1)} %segment_sums.1), channel_id=1, replica_groups=mesh['seg'=16,'band'=32] {'seg'}, dimensions={0} | all-to-all | bytes 262144 | tf_op jit(solution)/shard_map/all_to_all | solution.py:339
  28.5 0.6 %pad_maximum_fusion = f32[32,256]{1,0:T(8,128)} fusion(f32[32,128]{1,0:T(8,128)S(1)} %get-tuple-element.14, f32[32,128]{1,0:T(8,128)S(1)} %get-tuple-element.13), kind=kLoop, calls=%fused_computation.1 | loop fusion | flops 8192 | bytes 65536 | tf_op jit(solution)/shard_map/concatenate | solution.py:341
  (3 shorter events, 0.0 us)
Async XLA Ops:
  3.0 5.9 %collective-permute-start = (bf16[2,8,128]{2,1,0:T(8,128)(2,1)S(1)}, bf16[2,8,128]{2,1,0:T(8,128)(2,1)S(1)}, u32[]{:S(2)}, u32[]{:S(2)}) collective-permute-start(bf16[2,8,128]{2,1,0:T(8,128)(2,1)S(1)} %fusion), channel_id=1, source_target_pairs={{1,32},{32,1},{2,33},{33,2},{3,34},{34,3},{4,35},{35,4},{5,36},{36... | collective-permute-start | bytes 12296 | tf_op jit(solution)/shard_map/ppermute | solution.py:306
